TPU v7x, 32 devices: a whole 2x2x4 slice. The times are simulated.
32 devices in a mesh: ctx: 16 (over z, y, x), tp: 2 (over core).
Axes of the slice: x: 2, y: 2, z: 4, core: 2. Of those that a mesh axis runs over, the one named last changes fastest.
Arguments:
- tokens: bfloat16 [8192, 5120], P('ctx', 'tp'), may hold values from -6 to 6
- norm_gain: float32 [5120], replicated, may hold values from 0.1 to 1.9
- w_query: bfloat16 [5120, 5120], P('ctx', 'tp'), may hold values from -0.078125 to 0.078125
- cache_keys: bfloat16 [8192, 1024], P('ctx', 'tp'), may hold values from -100 to 100
- cache_values: bfloat16 [8192, 1024], P('ctx', 'tp'), may hold values from -6 to 6
- doc_start: int32 [8192], P('ctx'), may hold values from 0 to 8191, as said below
- tile_mask: int32 [64, 64], P('ctx'), may hold values from 0 to 1, as said below
Outputs:
- attended: bfloat16 [8192, 5120], P('ctx', 'tp')
Inputs may be any that keep to these rules, and one draw needn't show every extreme that they name: Documents are contiguous: doc_start is the same within a document and i - 2048 < doc_start[i] <= i; some document has exactly 2048 tokens. `tile_mask`: every diagonal tile is 1.
All inputs are finite; a program needn't handle non-finite values.
Results may differ from a plain program's by a relative error of at most 0.012.
The roundings to bfloat16 on the way count: a program that leaves them out, or rounds other values in their place, can miss the bound.
Values may be sent and summed in bfloat16 or wider, within the bound.
No kernel may reach another device: no remote copies, remote signals or barrier semaphores. Data moves between devices by JAX's collectives and lax.ppermute only.
A program may use at most 256 MiB of HBM per device.

v0:
```python
import math

import jax
import jax.numpy as jnp
from jax import lax
from jax.experimental import pallas as pl
from jax.experimental.pallas import tpu as pltpu
from jax.sharding import PartitionSpec as P

HD = 128
TILE = 128
MAXDOC = 2048
KEYS = 512
QUERIES = 256
CHUNKS = 4
FAR = 1 << 30
MASKED = -1e30


epsilon = 1e-05
exp2_scale = math.log2(math.e) / HD**0.5


def rows_kernel(counts, distances, shapes, info, marks_smem, marks_ref, *refs):
    parts, kv_count, halves, mask_width = counts
    tok_rows, shard_rows, source_rows = shapes
    n = len(distances)
    token_hbm = [refs[k * parts : (k + 1) * parts] for k in range(n)]
    w_hbm = refs[n * parts]
    kv_hbm = refs[n * parts + 1 :][:kv_count]
    out_hbm = refs[n * parts + 1 + kv_count :][:n]
    scratch = refs[n * parts + 1 + kv_count + n :]
    token_ref, w_ref, key_ref, value_ref, total_ref, query_ref, doc_full, acc_ref, max_ref, sum_ref, out_ref = scratch[:11]
    token_sem, w_sem, kv_sem, out_sem = scratch[11:]
    columns = w_ref.shape[1]
    heads = columns // HD
    depth = w_ref.shape[0]
    blocks = depth // source_rows
    swap = info[1]
    chunk = depth // CHUNKS
    chunks_part = CHUNKS // parts
    doc_rows = tok_rows // TILE
    window_rows = halves * kv_count * shard_rows
    base = window_rows - kv_count * shard_rows

    def token_copy(ref, at, c, slot):
        return pltpu.make_async_copy(
            ref.at[:, at * chunk : (at + 1) * chunk],
            token_ref.at[slot, :, c * chunk : (c + 1) * chunk],
            token_sem.at[slot, c],
        )

    def fetch_tokens(k, c):
        token_copy(token_hbm[k][c // chunks_part], c % chunks_part, c, k % 2).start()

    def rows_of(c):
        return lax.bitwise_xor(info[2], c // chunks_part) * chunks_part + c % chunks_part

    def w_copy(at, place):
        target = pl.ds(pl.multiple_of(place * source_rows, 16), source_rows)
        return pltpu.make_async_copy(w_hbm.at[at], w_ref.at[target], w_sem.at[place])

    blocks_chunk = blocks // CHUNKS

    def kv_copy(ref, half, which, place):
        target = pl.ds(pl.multiple_of(KEYS + place * shard_rows, 16), shard_rows)
        return pltpu.make_async_copy(
            ref.at[pl.ds((half * 2 + which) * shard_rows, shard_rows), :],
            (key_ref, value_ref)[which].at[target],
            kv_sem.at[place, which],
        )

    def out_copy(k, slot):
        return pltpu.make_async_copy(out_ref.at[slot], out_hbm[k], out_sem.at[slot])

    for c in range(CHUNKS):
        fetch_tokens(0, c)
        for at in range(blocks_chunk):
            place = rows_of(c) * blocks_chunk + at
            w_copy(lax.bitwise_xor(swap, place), place).start()
    for at in range(kv_count):
        for half in range(halves):
            for which in range(2):
                kv_copy(kv_hbm[at], half, which, half * kv_count + lax.bitwise_xor(swap, at)).start()
    key_ref[0:KEYS, :] = jnp.zeros((KEYS, HD), jnp.bfloat16)
    value_ref[0:KEYS, :] = jnp.zeros((KEYS, HD), jnp.bfloat16)

    stacked = heads * QUERIES
    subs = QUERIES // TILE

    def one_rows(k, carry):
        slot = lax.rem(k, 2)
        for ahead in range(1, n):

            @pl.when(k == ahead - 1)
            def _():
                for c in range(CHUNKS):
                    fetch_tokens(ahead, c)

        for c in range(CHUNKS):
            token_copy(token_hbm[0][0], 0, c, slot).wait()

            @pl.when(k == 0)
            def _():
                for at in range(blocks_chunk):
                    w_copy(0, rows_of(c) * blocks_chunk + at).wait()

            for first in range(0, tok_rows, QUERIES):
                piece = jnp.dot(
                    token_ref[slot, first : first + QUERIES, c * chunk : (c + 1) * chunk],
                    w_ref[pl.ds(pl.multiple_of(rows_of(c) * chunk, 16), chunk), :],
                    preferred_element_type=jnp.float32,
                )
                if c == 0:
                    total_ref[first : first + QUERIES, :] = piece
                else:
                    total_ref[first : first + QUERIES, :] += piece
        for tile in range(tok_rows // QUERIES):
            for head in range(heads):
                at = (tile * heads + head) * QUERIES
                query_ref[at : at + QUERIES, :] = total_ref[
                    tile * QUERIES : (tile + 1) * QUERIES, head * HD : (head + 1) * HD
                ].astype(jnp.bfloat16)

        @pl.when(k == 0)
        def _():
            for place in range(kv_count * halves):
                for which in range(2):
                    kv_copy(kv_hbm[0], 0, which, place).wait()

        @pl.when(k >= 2)
        def _():
            out_copy(0, slot).wait()

        distance = jnp.int32(distances[0])
        for other in range(1, n):
            distance = jnp.where(k == other, distances[other], distance)
        rows_first = base + lax.bitwise_xor(swap, distance) * tok_rows

        def one_tile(tile, carry):
            query = query_ref[pl.ds(pl.multiple_of(tile * stacked, stacked), stacked), :]
            row_first = rows_first + tile * QUERIES
            end = row_first + QUERIES
            for sub in range(subs):
                docs_row = marks_ref[distance, pl.ds(tile * subs + sub, 1), :].astype(jnp.float32)
                doc_full[sub] = jnp.transpose(jnp.broadcast_to(docs_row, (TILE, TILE))).astype(jnp.int32)
            first_key = marks_smem[distance, tile * subs, 0] - info[0]
            count = (end - first_key + KEYS - 1) // KEYS

            def one_block(back, carry):
                start = end - (back + 1) * KEYS
                at = pl.multiple_of(start + KEYS, TILE)
                keys = key_ref[pl.ds(at, KEYS), :]
                values = value_ref[pl.ds(at, KEYS), :]
                key_tile = (info[0] + start) // TILE
                lane = lax.broadcasted_iota(jnp.int32, (TILE, TILE), 1)
                row = lax.broadcasted_iota(jnp.int32, (TILE, TILE), 0)
                bias_rows = []
                for sub in range(subs):
                    causal = row + (row_first + sub * TILE - start)
                    docs = doc_full[sub] - (info[0] + start)
                    pieces = []
                    for m in range(KEYS // TILE):
                        column = lax.min(lax.max(key_tile + m, 0), mask_width - 1)
                        flat = (tile * subs + sub) * mask_width + column
                        shut = jnp.where(marks_smem[distance, doc_rows + flat // TILE, lax.rem(flat, TILE)] == 1, 0, FAR)
                        seen = (lane <= causal - m * TILE) & (lane >= docs + (shut - m * TILE))
                        pieces.append(jnp.where(seen, 0.0, MASKED))
                    bias_rows.append(jnp.concatenate(pieces, axis=1))
                bias = jnp.concatenate(bias_rows, axis=0)
                spans = [slice(head * QUERIES, (head + 1) * QUERIES) for head in range(heads)]
                scores = [
                    bias
                    + lax.dot_general(
                        query[span], keys, (((1,), (1,)), ((), ())), preferred_element_type=jnp.float32
                    )
                    for span in spans
                ]
                olds = [max_ref[span, :] for span in spans]
                news = [jnp.maximum(old, jnp.max(x, axis=1, keepdims=True)) for old, x in zip(olds, scores)]
                for span, x, old, new in zip(spans, scores, olds, news):
                    alpha = jnp.exp2((old - new) * exp2_scale)
                    shift = jnp.concatenate([new * exp2_scale] * (KEYS // HD), axis=1)
                    weights = jnp.exp2(x * exp2_scale - shift)
                    max_ref[span, :] = new
                    folded = weights[:, :HD]
                    for m in range(1, KEYS // HD):
                        folded = folded + weights[:, m * HD : (m + 1) * HD]
                    sum_ref[span, :] = sum_ref[span, :] * alpha + folded
                    product = jnp.dot(weights.astype(jnp.bfloat16), values, preferred_element_type=jnp.float32)
                    acc_ref[span, :] = acc_ref[span, :] * alpha + product
                return carry

            max_ref[...] = jnp.full(max_ref.shape, MASKED, jnp.float32)
            sum_ref[...] = jnp.zeros(sum_ref.shape, jnp.float32)
            acc_ref[...] = jnp.zeros(acc_ref.shape, jnp.float32)
            lax.fori_loop(0, count, one_block, 0)
            result = acc_ref[...] / jnp.sum(sum_ref[...], axis=1, keepdims=True)
            for head in range(heads):
                out_ref[slot, pl.ds(pl.multiple_of(tile * QUERIES, QUERIES), QUERIES), head * HD : (head + 1) * HD] = (
                    result[head * QUERIES : (head + 1) * QUERIES].astype(out_ref.dtype)
                )
            return carry

        lax.fori_loop(0, tok_rows // QUERIES, one_tile, 0)
        for at in range(n):

            @pl.when(k == at)
            def _():
                out_copy(at, at % 2).start()

        return carry

    lax.fori_loop(0, n, one_rows, 0)
    for k in range(max(n - 2, 0), n):
        out_copy(k, k % 2).wait()


def attend(info, marks, distances, token_parts, w_blocks, kv_parts, halves, mask_width):
    n = len(distances)
    parts = len(token_parts[0])
    rows = token_parts[0][0].shape[0]
    source_rows, columns = w_blocks.shape[1:]
    depth = w_blocks.shape[0] * source_rows
    heads = columns // HD
    shard_rows = kv_parts[0].shape[0] // (2 * halves) // TILE * TILE
    shards = len(kv_parts) * halves
    vmem = pl.BlockSpec(memory_space=pltpu.VMEM)
    smem = pl.BlockSpec(memory_space=pltpu.SMEM)
    leave = pl.BlockSpec(memory_space=pl.ANY)
    arrays = [part for block in token_parts for part in block] + [w_blocks] + list(kv_parts)
    counts = (parts, len(kv_parts), halves, mask_width)
    tile_rows = heads * QUERIES

    def kernel(*refs):
        rows_kernel(counts, distances, (rows, shard_rows, source_rows), *refs)

    return pl.pallas_call(
        kernel,
        out_shape=[jax.ShapeDtypeStruct((rows, columns), jnp.bfloat16)] * n,
        in_specs=[smem, smem, vmem] + [leave] * len(arrays),
        out_specs=[leave] * n,
        scratch_shapes=[
            pltpu.VMEM((2, rows, depth), jnp.bfloat16),
            pltpu.VMEM((depth, columns), jnp.bfloat16),
            pltpu.VMEM((KEYS + shards * shard_rows, HD), jnp.bfloat16),
            pltpu.VMEM((KEYS + shards * shard_rows, HD), jnp.bfloat16),
            pltpu.VMEM((rows, columns), jnp.float32),
            pltpu.VMEM((rows * heads, HD), jnp.bfloat16),
            pltpu.VMEM((QUERIES // TILE, TILE, TILE), jnp.int32),
            pltpu.VMEM((tile_rows, HD), jnp.float32),
            pltpu.VMEM((tile_rows, HD), jnp.float32),
            pltpu.VMEM((tile_rows, HD), jnp.float32),
            pltpu.VMEM((2, rows, columns), jnp.bfloat16),
            pltpu.SemaphoreType.DMA((2, CHUNKS)),
            pltpu.SemaphoreType.DMA((w_blocks.shape[0],)),
            pltpu.SemaphoreType.DMA((shards, 2)),
            pltpu.SemaphoreType.DMA((2,)),
        ],
        compiler_params=pltpu.CompilerParams(vmem_limit_bytes=60 << 20),
        cost_estimate=pl.CostEstimate(
            flops=n * (2 * rows * depth * columns + 4 * rows * columns * 1024),
            bytes_accessed=2 * (n * rows * depth + depth * columns + shards * 2 * shard_rows * HD + n * rows * columns),
            transcendentals=n * rows * heads * 1024,
        ),
    )(info, marks, marks, *arrays)


def marks_of(doc_start, tile_mask):
    return jnp.concatenate([doc_start.reshape(-1, TILE), tile_mask.reshape(-1, TILE)])


def planar(tokens, norm_gain, w_query, cache_keys, cache_values, doc_start, tile_mask, group):
    devices = lax.axis_size("ctx")
    index = lax.axis_index("ctx")
    core = lax.axis_index("tp")
    place = lax.rem(index, group)
    tok_rows, width = tokens.shape
    kv_width = cache_keys.shape[1] // group
    q_width = w_query.shape[1] // group
    rows = group * tok_rows
    lines = [[first + k for first in range(0, devices, group)] for k in range(group)]
    far = range(1, group)

    def swapped(block, distance):
        return lax.ppermute(block, "ctx", [(i, i ^ distance) for i in range(devices)])

    def other_core(block):
        return lax.ppermute(block, "tp", [(0, 1), (1, 0)])

    def columns_for(array, distance, first, size, of, axis):
        at = lax.bitwise_xor(place, distance) * of + first
        return lax.dynamic_slice_in_dim(array, at, size, axis)

    def after(values, *earlier):
        flat = lax.optimization_barrier((tuple(values), tuple(earlier)))
        return list(flat[0])

    first_columns = (q_width // HD + 1) // 2 * HD
    cuts = ((0, first_columns), (first_columns, q_width))

    w_cut = [columns_for(w_query, d, 0, q_width, q_width, 1) for d in range(group)]
    w_plane = w_cut[:1] + [swapped(w_cut[d], d) for d in far]
    float_tokens = tokens.astype(jnp.float32)
    squares = jnp.sum(float_tokens * float_tokens, axis=-1)
    squares = squares + other_core(squares)
    inverse = lax.rsqrt(squares / (2 * width) + epsilon)
    gain = lax.dynamic_slice_in_dim(norm_gain, core * width, width, 0)
    normed = (float_tokens * inverse[:, None] * gain).astype(jnp.bfloat16)

    w_plane = after(w_plane, normed)
    w_stacks = [jnp.stack([block[:, low:high] for block in w_plane]) for low, high in cuts]
    w_chunks = [lax.all_gather(w_stacks[0], "ctx", axis=0, tiled=True, axis_index_groups=lines)]

    (keys_later,) = after([cache_keys], w_stacks[0])
    kv_own = jnp.stack([keys_later, cache_values])
    kv_before = lax.ppermute(kv_own, "ctx", [(i, i + group) for i in range(devices - group)])

    marks_own = marks_of(doc_start, tile_mask)
    marks_rows = marks_own.shape[0]
    bytes_own = jnp.concatenate([marks_own >> 16, (marks_own >> 8) & 255, marks_own & 255]).astype(jnp.bfloat16)
    bytes_own = jnp.pad(bytes_own, ((0, -bytes_own.shape[0] % 16), (0, 0)))

    def kv_for(d):
        cut = [columns_for(array, d, 0, kv_width, kv_width, 2).reshape(-1, kv_width) for array in (kv_before, kv_own)]
        return jnp.concatenate(cut + [bytes_own])

    kv_cut = after([kv_for(d) for d in range(group)], w_stacks[1])
    kv_parts = kv_cut[:1] + [swapped(kv_cut[d], d) for d in far]

    sent = jnp.stack([part[4 * tok_rows :] for part in kv_parts]).astype(jnp.int32)
    marks = sent[:, :marks_rows] * 65536 + sent[:, marks_rows : 2 * marks_rows] * 256
    marks = marks + sent[:, 2 * marks_rows : 3 * marks_rows]
    from_x, from_y = swapped(normed, 1), swapped(normed, 2)
    mine_other = other_core(normed)
    (w_after,) = after([w_stacks[1]], *kv_parts)
    w_chunks.append(lax.all_gather(w_after, "ctx", axis=0, tiled=True, axis_index_groups=lines))

    half = width // 2
    relay_y, relay_x = from_y[:, :half], from_x[:, half:]
    from_x, from_y, relay_y, relay_x = after([from_x, from_y, relay_y, relay_x], *kv_parts)
    corner_a, corner_b = swapped(relay_y, 1), swapped(relay_x, 2)
    token_parts = [[normed, mine_other]] + [[from_x, other_core(from_x)], [from_y, other_core(from_y)]]

    info = jnp.stack([(index // group - 1) * rows, place, core]).astype(jnp.int32)
    width_mask = tile_mask.shape[1]

    def call(distances, chunk, *earlier):
        chosen = [token_parts[d] for d in distances]
        (start,) = after([info], *earlier)
        return attend(start, marks, distances, chosen, chunk, kv_parts, 2, width_mask)

    pieces, last = {}, ()
    for chunk, distances in ((0, (2, 1, 0)), (0, (3,)), (1, (3, 2, 1)), (1, (0,))):
        if distances == (3,):
            corner = jnp.concatenate(after([corner_a, corner_b], *last), axis=1)
            token_parts.append([corner, other_core(corner)])
        outs = call(distances, w_chunks[chunk], *last)
        last = outs[:1]
        pieces.update({(d, chunk): swapped(out, d) if d else out for d, out in zip(distances, outs)})
    return joined(info, pieces, q_width, [low for low, _ in cuts], group * q_width)


def joined(info, pieces, q_width, lows, columns):
    keys = sorted(pieces)
    rows = pieces[keys[0]].shape[0]
    vmem = pl.BlockSpec(memory_space=pltpu.VMEM)

    def kernel(info_ref, *refs):
        out_ref = refs[-1]
        for k, (distance, chunk) in enumerate(keys):
            at = pl.multiple_of(lax.bitwise_xor(info_ref[1], distance) * q_width + lows[chunk], HD)
            out_ref[:, pl.ds(at, refs[k].shape[1])] = refs[k][...]

    return pl.pallas_call(
        kernel,
        out_shape=jax.ShapeDtypeStruct((rows, columns), jnp.bfloat16),
        in_specs=[pl.BlockSpec(memory_space=pltpu.SMEM)] + [vmem] * len(keys),
        out_specs=vmem,
        cost_estimate=pl.CostEstimate(flops=0, bytes_accessed=4 * rows * columns, transcendentals=0),
    )(info, *[pieces[key] for key in keys])


def plain(tokens, norm_gain, w_query, cache_keys, cache_values, doc_start, tile_mask):
    devices = lax.axis_size("ctx")
    index = lax.axis_index("ctx")
    tok_rows = tokens.shape[0]
    float_tokens = lax.all_gather(tokens, "tp", axis=1, tiled=True).astype(jnp.float32)
    inverse = lax.rsqrt(jnp.mean(float_tokens * float_tokens, axis=-1, keepdims=True) + epsilon)
    normed = (float_tokens * inverse * norm_gain).astype(jnp.bfloat16)
    kv_heads = cache_keys.shape[1] // HD
    q_width = w_query.shape[1] // kv_heads
    w_blocks = lax.all_gather(w_query, "ctx", axis=0)
    reach = (MAXDOC + tok_rows - 2) // tok_rows
    kv_own = jnp.stack([cache_keys, cache_values])
    shards = [
        lax.ppermute(kv_own, "ctx", [(i, i + distance) for i in range(devices - distance)])
        for distance in range(reach, 0, -1)
    ]
    kv_window = jnp.stack(shards + [kv_own])
    info = jnp.stack([(index - reach) * tok_rows, jnp.int32(0), jnp.int32(0)]).astype(jnp.int32)
    marks = marks_of(doc_start, tile_mask)[None]
    outs = [
        attend(
            info,
            marks,
            (0,),
            [[normed]],
            w_blocks[:, :, head * q_width : (head + 1) * q_width],
            [kv_window[:, :, :, head * HD : (head + 1) * HD].reshape(-1, HD)],
            reach + 1,
            tile_mask.shape[1],
        )[0]
        for head in range(kv_heads)
    ]
    return outs[0] if kv_heads == 1 else jnp.concatenate(outs, axis=1)


def on_device(*arrays):
    kv_heads = arrays[3].shape[1] // HD
    group = 4
    rows = group * arrays[0].shape[0]
    if kv_heads == group and lax.axis_size("ctx") % group == 0 and lax.axis_size("tp") == 2 and rows >= MAXDOC - 1:
        return planar(*arrays, group)
    return plain(*arrays)


def solution(mesh):
    return jax.shard_map(
        on_device,
        mesh=mesh,
        in_specs=(
            P("ctx", "tp"),
            P(),
            P("ctx", "tp"),
            P("ctx", "tp"),
            P("ctx", "tp"),
            P("ctx"),
            P("ctx", None),
        ),
        out_specs=P("ctx", "tp"),
        check_vma=False,
    )
```

profile of v0, /device:TPU:0, one launch (start us, length us, event | category | flops | bytes accessed | tf_op | source)
XLA Modules:
  0.0 237.5 jit_solution(2759357430639033110)
XLA Ops:
  6.5 2.5 %fusion = f32[512]{0:T(512)S(1)} fusion(bf16[512,2560]{1,0:T(8,128)(2,1)} %param.7), kind=kLoop, calls=%fused_computation.2 | loop fusion | flops 3931648 | bytes 2623488 | tf_op jit(solution)/shard_map/reduce_sum | solution.py:305
  9.5 2.5 %constant_dynamic-slice_fusion.4 = (bf16[320,640]{1,0:T(8,128)(2,1)}, bf16[320,640]{1,0:T(8,128)(2,1)}, bf16[320,640]{1,0:T(8,128)(2,1)S(1)}, bf16[320,640]{1,0:T(8,128)(2,1)}) fusion(bf16[320,2560]{1,0:T(8,128)(2,1)} %param.9, s32[]{:T(128)S(6)} %select_n.40, s32[]{:T(128)S(6)} %select_n.38, s32[]{:T(128)S(6)} %select_n.37, s32[]{:T(128)S(6)} %select_n.39), kind=kLoop, calls=%fused_computation.59 | loop fusion | bytes 3276816 | tf_op jit(solution)/shard_map/dynamic_slice | solution.py:293
  12.0 2.5 %collective-permute-start = (bf16[320,640]{1,0:T(8,128)(2,1)}, bf16[320,640]{1,0:T(8,128)(2,1)}, u32[]{:S(2)}, u32[]{:S(2)}) collective-permute-start(bf16[320,640]{1,0:T(8,128)(2,1)} %get-tuple-element.56), channel_id=1, source_target_pairs={{0,2},{2,0},{4,6},{6,4},{8,10},{10,8},{12,14},{14,12},{16,18},{18,... | collective-permute-start | bytes 1228808 | tf_op jit(solution)/shard_map/ppermute | solution.py:286
  14.5 1.5 collective-permute-start.1
  16.2 2.2 fusion.2.refs_7_.refs_3_
  18.3 6.8 %collective-permute-done = bf16[320,640]{1,0:T(8,128)(2,1)} collective-permute-done((bf16[320,640]{1,0:T(8,128)(2,1)}, bf16[320,640]{1,0:T(8,128)(2,1)}, u32[]{:S(2)}, u32[]{:S(2)}) %collective-permute-start) | collective-permute-done | bytes 409632 | tf_op jit(solution)/shard_map/ppermute | solution.py:286
  25.2 10.0 %collective-permute-done.1 = bf16[320,640]{1,0:T(8,128)(2,1)} collective-permute-done((bf16[320,640]{1,0:T(8,128)(2,1)}, bf16[320,640]{1,0:T(8,128)(2,1)}, u32[]{:S(2)}, u32[]{:S(2)}) %collective-permute-start.1) | collective-permute-done | bytes 409632 | tf_op jit(solution)/shard_map/ppermute | solution.py:286
  38.6 1.6 collective-permute-start.9
  40.7 2.1 pad_maximum_fusion
  42.8 4.5 %collective-permute-start.4 = (bf16[2,512,512]{2,1,0:T(8,128)(2,1)}, bf16[2,512,512]{2,1,0:T(8,128)(2,1)}, u32[]{:S(2)}, u32[]{:S(2)}) collective-permute-start(bf16[2,512,512]{2,1,0:T(8,128)(2,1)} %pad_maximum_fusion), channel_id=1, source_target_pairs={{0,8},{2,10},{4,12},{6,14},{8,16},{10,18},{12,20},{14,22},{16,24},... | collective-permute-start | bytes 3145736 | tf_op jit(solution)/shard_map/ppermute | solution.py:317
  54.0 36.4 %collective-permute-done.4 = bf16[2,512,512]{2,1,0:T(8,128)(2,1)} collective-permute-done((bf16[2,512,512]{2,1,0:T(8,128)(2,1)}, bf16[2,512,512]{2,1,0:T(8,128)(2,1)}, u32[]{:S(2)}, u32[]{:S(2)}) %collective-permute-start.4) | collective-permute-done | bytes 1048608 | tf_op jit(solution)/shard_map/ppermute | solution.py:317
  90.4 1.3 constant_dynamic-slice_fusion
  92.9 2.5 %collective-permute-start.6 = (bf16[2080,128]{1,0:T(8,128)(2,1)S(1)}, bf16[2080,128]{1,0:T(8,128)(2,1)}, u32[]{:S(2)}, u32[]{:S(2)}) collective-permute-start(bf16[2080,128]{1,0:T(8,128)(2,1)S(1)} %get-tuple-element.37), channel_id=1, source_target_pairs={{0,4},{2,6},{4,0},{6,2},{8,12},{10,14},{12,8},{14,10},{16,20},{18,... | collective-permute-start | bytes 1597448 | tf_op jit(solution)/shard_map/ppermute | solution.py:286
  96.1 12.3 %collective-permute-done.9.refs_3_.refs_5_ = bf16[512,2560]{1,0:T(8,128)(2,1)} collective-permute-done((bf16[512,2560]{1,0:T(8,128)(2,1)S(1)}, bf16[512,2560]{1,0:T(8,128)(2,1)}, u32[]{:S(2)}, u32[]{:S(2)}) %collective-permute-start.9) | collective-permute-done | bytes 2621472 | tf_op jit(solution)/shard_map/ppermute | solution.py:286
  108.4 2.5 %slice.71 = bf16[512,1280]{1,0:T(8,128)(2,1)} slice(bf16[512,2560]{1,0:T(8,128)(2,1)} %collective-permute-done.9.refs_3_.refs_5_), slice={[0:512], [0:1280]} | slice | bytes 2621440 | tf_op jit(solution)/shard_map/slice | solution.py:340
  110.9 2.5 %slice.72 = bf16[512,1280]{1,0:T(8,128)(2,1)} slice(bf16[512,2560]{1,0:T(8,128)(2,1)} %collective-permute-done.8.refs_5_.refs_7_), slice={[0:512], [1280:2560]} | slice | bytes 2621440 | tf_op jit(solution)/shard_map/slice | solution.py:340
  113.4 6.4 %collective-permute-done.6.refs_12_.refs_8_ = bf16[2080,128]{1,0:T(8,128)(2,1)} collective-permute-done((bf16[2080,128]{1,0:T(8,128)(2,1)S(1)}, bf16[2080,128]{1,0:T(8,128)(2,1)}, u32[]{:S(2)}, u32[]{:S(2)}) %collective-permute-start.6) | collective-permute-done | bytes 532512 | tf_op jit(solution)/shard_map/ppermute | solution.py:286
  123.3 1.5 collective-permute-start.14
  126.8 3.1 %collective-permute-done.11.refs_6_.refs_8_ = bf16[512,2560]{1,0:T(8,128)(2,1)} collective-permute-done((bf16[512,2560]{1,0:T(8,128)(2,1)}, bf16[512,2560]{1,0:T(8,128)(2,1)}, u32[]{:S(2)}, u32[]{:S(2)}) %collective-permute-start.11) | collective-permute-done | bytes 2621472 | tf_op jit(solution)/shard_map/ppermute | solution.py:289
  130.0 1.6 all-gather.3.cloned.1.call-done.refs_9_.refs_5_
  131.6 27.2 %shard_map.73 = (bf16[512,384]{1,0:T(8,128)(2,1)}, bf16[512,384]{1,0:T(8,128)(2,1)}, bf16[512,384]{1,0:T(8,128)(2,1)}) custom-call(s32[3]{0:T(128)} %pad_add_fusion.1.refs_0_.info_ref, s32[4,6,128]{2,1,0:T(8,128)} %fusion.8.refs_1_.refs_2_, s32[4,6,128]{2,1,0:T(8,128)} %fusion.8.refs_1_.refs_2_, bf16[512,2560]{1,0:T(8,128)(2,1)} %collective-permute-done.9.refs_3_.refs_5_, ...), custom_call_target="tpu_custom_call" | custom-call | flops 8455716864 | bytes 22937600 | tf_op jit(solution)/shard_map/pallas_call | solution.py:238
  158.8 1.4 constant_dynamic-update-slice_fusion.1
  160.3 1.4 constant_dynamic-update-slice_fusion.refs_3_
  161.8 4.7 %collective-permute-start.18 = (bf16[512,384]{1,0:T(8,128)(2,1)}, bf16[512,384]{1,0:T(8,128)(2,1)S(1)}, u32[]{:S(2)}, u32[]{:S(2)}) collective-permute-start(bf16[512,384]{1,0:T(8,128)(2,1)} %get-tuple-element.42), channel_id=1, source_target_pairs={{0,4},{2,6},{4,0},{6,2},{8,12},{10,14},{12,8},{14,10},{16,20},{18,... | collective-permute-start | bytes 1179656 | tf_op jit(solution)/shard_map/ppermute | solution.py:286
  166.5 2.2 collective-permute-start.16
  168.8 15.6 %shard_map.74 = bf16[512,384]{1,0:T(8,128)(2,1)} custom-call(s32[3]{0:T(128)} %pad_add_fusion.1.refs_0_.info_ref, s32[4,6,128]{2,1,0:T(8,128)} %fusion.8.refs_1_.refs_2_, s32[4,6,128]{2,1,0:T(8,128)} %fusion.8.refs_1_.refs_2_, bf16[512,2560]{1,0:T(8,128)(2,1)} %copy-done.2, bf16[512,2560]{1,0:T(8,128)(2,1)} %collective-permute-done.15.refs_4_, ...), custom_call_target="tpu_custom_call" | custom-call | flops 2818572288 | bytes 11665408 | tf_op jit(solution)/shard_map/pallas_call | solution.py:238
  184.4 4.7 %all-gather.5.cloned.1.call-done.refs_9_.refs_5_ = bf16[16,320,256]{2,1,0:T(8,128)(2,1)} async-done(((bf16[4,320,256]{2,1,0:T(8,128)(2,1)}), bf16[16,320,256]{2,1,0:T(8,128)(2,1)}) %all-gather.5.cloned.1.call-update) | async-done | bytes 2621456 | tf_op jit(solution)/shard_map/all_gather | solution.py:337
  189.1 23.2 %shard_map.75 = (bf16[512,256]{1,0:T(8,128)(2,1)}, bf16[512,256]{1,0:T(8,128)(2,1)}, bf16[512,256]{1,0:T(8,128)(2,1)}) custom-call(s32[3]{0:T(128)} %pad_add_fusion.1.refs_0_.info_ref, s32[4,6,128]{2,1,0:T(8,128)} %fusion.8.refs_1_.refs_2_, s32[4,6,128]{2,1,0:T(8,128)} %fusion.8.refs_1_.refs_2_, bf16[512,2560]{1,0:T(8,128)(2,1)} %copy-done.2, ...), custom_call_target="tpu_custom_call" | custom-call | flops 5637144576 | bytes 21233664 | tf_op jit(solution)/shard_map/pallas_call | solution.py:238
  212.6 3.3 %collective-permute-start.21 = (bf16[512,256]{1,0:T(8,128)(2,1)}, bf16[512,256]{1,0:T(8,128)(2,1)S(1)}, u32[]{:S(2)}, u32[]{:S(2)}) collective-permute-start(bf16[512,256]{1,0:T(8,128)(2,1)} %get-tuple-element.50), channel_id=1, source_target_pairs={{0,6},{2,4},{4,2},{6,0},{8,14},{10,12},{12,10},{14,8},{16,22},{18,... | collective-permute-start | bytes 786440 | tf_op jit(solution)/shard_map/ppermute | solution.py:286
  215.9 8.3 %shard_map.76.refs_1_ = bf16[512,256]{1,0:T(8,128)(2,1)} custom-call(s32[3]{0:T(128)} %pad_add_fusion.1.refs_0_.info_ref, s32[4,6,128]{2,1,0:T(8,128)} %fusion.8.refs_1_.refs_2_, s32[4,6,128]{2,1,0:T(8,128)} %fusion.8.refs_1_.refs_2_, bf16[512,2560]{1,0:T(8,128)(2,1)} %fusion.2.refs_7_.refs_3_, bf16[512,2560]{1,0:T(8,128)(2,1)} %collective-permute-done.12.refs_8_.refs_4_, ...), custom_call_target="tpu_custom_call" | custom-call | flops 1879048192 | bytes 10223616 | tf_op jit(solution)/shard_map/pallas_call | solution.py:238
  224.3 2.0 collective-permute-done.19.refs_5_
  227.3 3.4 %shard_map.77 = bf16[512,2560]{1,0:T(8,128)(2,1)} custom-call(s32[3]{0:T(128)} %pad_add_fusion.1.refs_0_.info_ref, bf16[512,384]{1,0:T(8,128)(2,1)} %get-tuple-element.41.refs_0_, bf16[512,256]{1,0:T(8,128)(2,1)} %shard_map.76.refs_1_, bf16[512,384]{1,0:T(8,128)(2,1)} %copy-done.6, bf16[512,256]{1,0:T(8,128)(2,1)} %copy-done.8, bf16[512,384]{1,0:T(8,128)(2,1)} %copy-done.5, ...), custom_call_target="tpu_custom_call" | custom-call | bytes 5242880 | tf_op jit(solution)/shard_map/pallas_call | solution.py:375
  (75 shorter events, 20.1 us)
Async XLA Ops:
  6.5 9.6 %copy-start = (bf16[512,2560]{1,0:T(8,128)(2,1)S(1)}, bf16[512,2560]{1,0:T(8,128)(2,1)}, u32[]{:S(2)}) copy-start(bf16[512,2560]{1,0:T(8,128)(2,1)} %param.7) | copy-start | bytes 7864324
  6.5 9.5 %copy-start.11 = (f32[5120]{0:T(1024)S(1)}, f32[5120]{0:T(1024)}, u32[]{:S(2)}) copy-start(f32[5120]{0:T(1024)} %param.8) | copy-start | bytes 61444
  6.5 125.0 %all-gather.3.cloned.1.call-start = ((), (), s32[]{:S(2)}) async-start(), calls=%async_computation | async-start | bytes 4915200 | tf_op jit(solution)/shard_map/all_gather | solution.py:313
  9.0 7.1 %collective-permute-start.3 = (f32[512]{0:T(512)S(1)}, f32[512]{0:T(512)S(1)}, u32[]{:S(2)}, u32[]{:S(2)}) collective-permute-start(f32[512]{0:T(512)S(1)} %fusion), channel_id=1, source_target_pairs={{0,1},{1,0},{2,3},{3,2},{4,5},{5,4},{6,7},{7,6},{8,9},{9,8},{10,11... | collective-permute-start | bytes 6152 | tf_op jit(solution)/shard_map/ppermute | solution.py:289
  12.0 13.2 %collective-permute-start = (bf16[320,640]{1,0:T(8,128)(2,1)}, bf16[320,640]{1,0:T(8,128)(2,1)}, u32[]{:S(2)}, u32[]{:S(2)}) collective-permute-start(bf16[320,640]{1,0:T(8,128)(2,1)} %get-tuple-element.56), channel_id=1, source_target_pairs={{0,2},{2,0},{4,6},{6,4},{8,10},{10,8},{12,14},{14,12},{16,18},{18,... | collective-permute-start | bytes 1228808 | tf_op jit(solution)/shard_map/ppermute | solution.py:286
  14.5 20.6 %collective-permute-start.1 = (bf16[320,640]{1,0:T(8,128)(2,1)}, bf16[320,640]{1,0:T(8,128)(2,1)}, u32[]{:S(2)}, u32[]{:S(2)}) collective-permute-start(bf16[320,640]{1,0:T(8,128)(2,1)} %get-tuple-element.58), channel_id=1, source_target_pairs={{0,4},{2,6},{4,0},{6,2},{8,12},{10,14},{12,8},{14,10},{16,20},{18,... | collective-permute-start | bytes 1228808 | tf_op jit(solution)/shard_map/ppermute | solution.py:286
  16.1 19.1 %collective-permute-start.2 = (bf16[320,640]{1,0:T(8,128)(2,1)}, bf16[320,640]{1,0:T(8,128)(2,1)}, u32[]{:S(2)}, u32[]{:S(2)}) collective-permute-start(bf16[320,640]{1,0:T(8,128)(2,1)} %get-tuple-element.55), channel_id=1, source_target_pairs={{0,6},{2,4},{4,2},{6,0},{8,14},{10,12},{12,10},{14,8},{16,22},{18,... | collective-permute-start | bytes 1228808 | tf_op jit(solution)/shard_map/ppermute | solution.py:286
  18.3 20.2 %copy-start.1 = (bf16[512,2560]{1,0:T(8,128)(2,1)S(1)}, bf16[512,2560]{1,0:T(8,128)(2,1)}, u32[]{:S(2)}) copy-start(bf16[512,2560]{1,0:T(8,128)(2,1)} %fusion.2.refs_7_.refs_3_) | copy-start | bytes 7864324
  18.3 22.4 %copy-start.4 = (bf16[512,512]{1,0:T(8,128)(2,1)S(1)}, bf16[512,512]{1,0:T(8,128)(2,1)}, u32[]{:S(2)}) copy-start(bf16[512,512]{1,0:T(8,128)(2,1)} %param.10) | copy-start | bytes 1572868
  38.5 150.6 %all-gather.5.cloned.1.call-start = ((), (), s32[]{:S(2)}) async-start(), calls=%async_computation.1 | async-start | bytes 3276800 | tf_op jit(solution)/shard_map/all_gather | solution.py:337
  38.6 69.9 %collective-permute-start.9 = (bf16[512,2560]{1,0:T(8,128)(2,1)S(1)}, bf16[512,2560]{1,0:T(8,128)(2,1)}, u32[]{:S(2)}, u32[]{:S(2)}) collective-permute-start(bf16[512,2560]{1,0:T(8,128)(2,1)S(1)} %copy-done.1), channel_id=1, source_target_pairs={{0,4},{2,6},{4,0},{6,2},{8,12},{10,14},{12,8},{14,10},{16,20},{18,... | collective-permute-start | bytes 7864328 | tf_op jit(solution)/shard_map/ppermute | solution.py:286
  40.2 70.8 %collective-permute-start.8 = (bf16[512,2560]{1,0:T(8,128)(2,1)S(1)}, bf16[512,2560]{1,0:T(8,128)(2,1)}, u32[]{:S(2)}, u32[]{:S(2)}) collective-permute-start(bf16[512,2560]{1,0:T(8,128)(2,1)S(1)} %copy-done.1), channel_id=1, source_target_pairs={{0,2},{2,0},{4,6},{6,4},{8,10},{10,8},{12,14},{14,12},{16,18},{18,... | collective-permute-start | bytes 7864328 | tf_op jit(solution)/shard_map/ppermute | solution.py:286
  42.8 47.6 %collective-permute-start.4 = (bf16[2,512,512]{2,1,0:T(8,128)(2,1)}, bf16[2,512,512]{2,1,0:T(8,128)(2,1)}, u32[]{:S(2)}, u32[]{:S(2)}) collective-permute-start(bf16[2,512,512]{2,1,0:T(8,128)(2,1)} %pad_maximum_fusion), channel_id=1, source_target_pairs={{0,8},{2,10},{4,12},{6,14},{8,16},{10,18},{12,20},{14,22},{16,24},... | collective-permute-start | bytes 3145736 | tf_op jit(solution)/shard_map/ppermute | solution.py:317
  92.6 29.5 %copy-start.3 = (bf16[2080,128]{1,0:T(8,128)(2,1)}, bf16[2080,128]{1,0:T(8,128)(2,1)S(1)}, u32[]{:S(2)}) copy-start(bf16[2080,128]{1,0:T(8,128)(2,1)S(1)} %get-tuple-element.35.refs_10_.refs_6_) | copy-start | bytes 1597444
  92.6 20.8 %collective-permute-start.7 = (bf16[2080,128]{1,0:T(8,128)(2,1)S(1)}, bf16[2080,128]{1,0:T(8,128)(2,1)}, u32[]{:S(2)}, u32[]{:S(2)}) collective-permute-start(bf16[2080,128]{1,0:T(8,128)(2,1)S(1)} %get-tuple-element.38), channel_id=1, source_target_pairs={{0,6},{2,4},{4,2},{6,0},{8,14},{10,12},{12,10},{14,8},{16,22},{18,... | collective-permute-start | bytes 1597448 | tf_op jit(solution)/shard_map/ppermute | solution.py:286
  92.9 26.9 %collective-permute-start.6 = (bf16[2080,128]{1,0:T(8,128)(2,1)S(1)}, bf16[2080,128]{1,0:T(8,128)(2,1)}, u32[]{:S(2)}, u32[]{:S(2)}) collective-permute-start(bf16[2080,128]{1,0:T(8,128)(2,1)S(1)} %get-tuple-element.37), channel_id=1, source_target_pairs={{0,4},{2,6},{4,0},{6,2},{8,12},{10,14},{12,8},{14,10},{16,20},{18,... | collective-permute-start | bytes 1597448 | tf_op jit(solution)/shard_map/ppermute | solution.py:286
  95.3 25.6 %collective-permute-start.5 = (bf16[2080,128]{1,0:T(8,128)(2,1)S(1)}, bf16[2080,128]{1,0:T(8,128)(2,1)}, u32[]{:S(2)}, u32[]{:S(2)}) collective-permute-start(bf16[2080,128]{1,0:T(8,128)(2,1)S(1)} %get-tuple-element.36), channel_id=1, source_target_pairs={{0,2},{2,0},{4,6},{6,4},{8,10},{10,8},{12,14},{14,12},{16,18},{18,... | collective-permute-start | bytes 1597448 | tf_op jit(solution)/shard_map/ppermute | solution.py:286
  108.4 18.4 %collective-permute-start.12 = (bf16[512,2560]{1,0:T(8,128)(2,1)S(1)}, bf16[512,2560]{1,0:T(8,128)(2,1)}, u32[]{:S(2)}, u32[]{:S(2)}) collective-permute-start(bf16[512,2560]{1,0:T(8,128)(2,1)S(1)} %copy-done.1), channel_id=1, source_target_pairs={{0,1},{1,0},{2,3},{3,2},{4,5},{5,4},{6,7},{7,6},{8,9},{9,8},{10,11... | collective-permute-start | bytes 7864328 | tf_op jit(solution)/shard_map/ppermute | solution.py:289
  121.0 5.9 %collective-permute-start.10 = (bf16[512,2560]{1,0:T(8,128)(2,1)}, bf16[512,2560]{1,0:T(8,128)(2,1)}, u32[]{:S(2)}, u32[]{:S(2)}) collective-permute-start(bf16[512,2560]{1,0:T(8,128)(2,1)} %collective-permute-done.9.refs_3_.refs_5_), channel_id=1, source_target_pairs={{0,1},{1,0},{2,3},{3,2},{4,5},{5,4},{6,7},{7,6},{8,9},{9,8},{10,11... | collective-permute-start | bytes 7864328 | tf_op jit(solution)/shard_map/ppermute | solution.py:289
  121.0 9.0 %collective-permute-start.11 = (bf16[512,2560]{1,0:T(8,128)(2,1)}, bf16[512,2560]{1,0:T(8,128)(2,1)}, u32[]{:S(2)}, u32[]{:S(2)}) collective-permute-start(bf16[512,2560]{1,0:T(8,128)(2,1)} %collective-permute-done.8.refs_5_.refs_7_), channel_id=1, source_target_pairs={{0,1},{1,0},{2,3},{3,2},{4,5},{5,4},{6,7},{7,6},{8,9},{9,8},{10,11... | collective-permute-start | bytes 7864328 | tf_op jit(solution)/shard_map/ppermute | solution.py:289
  122.8 36.0 %collective-permute-start.13 = (bf16[512,1280]{1,0:T(8,128)(2,1)}, bf16[512,1280]{1,0:T(8,128)(2,1)}, u32[]{:S(2)}, u32[]{:S(2)}) collective-permute-start(bf16[512,1280]{1,0:T(8,128)(2,1)} %slice.71), channel_id=1, source_target_pairs={{0,2},{2,0},{4,6},{6,4},{8,10},{10,8},{12,14},{14,12},{16,18},{18,... | collective-permute-start | bytes 3932168 | tf_op jit(solution)/shard_map/ppermute | solution.py:286
  123.3 35.5 %collective-permute-start.14 = (bf16[512,1280]{1,0:T(8,128)(2,1)}, bf16[512,1280]{1,0:T(8,128)(2,1)}, u32[]{:S(2)}, u32[]{:S(2)}) collective-permute-start(bf16[512,1280]{1,0:T(8,128)(2,1)} %slice.72), channel_id=1, source_target_pairs={{0,4},{2,6},{4,0},{6,2},{8,12},{10,14},{12,8},{14,10},{16,20},{18,... | collective-permute-start | bytes 3932168 | tf_op jit(solution)/shard_map/ppermute | solution.py:286
  161.7 7.1 %copy-start.2 = (bf16[512,2560]{1,0:T(8,128)(2,1)}, bf16[512,2560]{1,0:T(8,128)(2,1)S(1)}, u32[]{:S(2)}) copy-start(bf16[512,2560]{1,0:T(8,128)(2,1)S(1)} %constant_dynamic-update-slice_fusion.refs_3_) | copy-start | bytes 7864324
  161.7 7.1 %collective-permute-start.15 = (bf16[512,2560]{1,0:T(8,128)(2,1)S(1)}, bf16[512,2560]{1,0:T(8,128)(2,1)}, u32[]{:S(2)}, u32[]{:S(2)}) collective-permute-start(bf16[512,2560]{1,0:T(8,128)(2,1)S(1)} %constant_dynamic-update-slice_fusion.refs_3_), channel_id=1, source_target_pairs={{0,1},{1,0},{2,3},{3,2},{4,5},{5,4},{6,7},{7,6},{8,9},{9,8},{10,11... | collective-permute-start | bytes 7864328 | tf_op jit(solution)/shard_map/ppermute | solution.py:289
  161.8 62.4 %collective-permute-start.18 = (bf16[512,384]{1,0:T(8,128)(2,1)}, bf16[512,384]{1,0:T(8,128)(2,1)S(1)}, u32[]{:S(2)}, u32[]{:S(2)}) collective-permute-start(bf16[512,384]{1,0:T(8,128)(2,1)} %get-tuple-element.42), channel_id=1, source_target_pairs={{0,4},{2,6},{4,0},{6,2},{8,12},{10,14},{12,8},{14,10},{16,20},{18,... | collective-permute-start | bytes 1179656 | tf_op jit(solution)/shard_map/ppermute | solution.py:286
  166.5 46.1 %collective-permute-start.16 = (bf16[512,384]{1,0:T(8,128)(2,1)}, bf16[512,384]{1,0:T(8,128)(2,1)S(1)}, u32[]{:S(2)}, u32[]{:S(2)}) collective-permute-start(bf16[512,384]{1,0:T(8,128)(2,1)} %get-tuple-element.52), channel_id=1, source_target_pairs={{0,2},{2,0},{4,6},{6,4},{8,10},{10,8},{12,14},{14,12},{16,18},{18,... | collective-permute-start | bytes 1179656 | tf_op jit(solution)/shard_map/ppermute | solution.py:286
  184.3 42.0 %collective-permute-start.20 = (bf16[512,384]{1,0:T(8,128)(2,1)}, bf16[512,384]{1,0:T(8,128)(2,1)S(1)}, u32[]{:S(2)}, u32[]{:S(2)}) collective-permute-start(bf16[512,384]{1,0:T(8,128)(2,1)} %shard_map.74), channel_id=1, source_target_pairs={{0,6},{2,4},{4,2},{6,0},{8,14},{10,12},{12,10},{14,8},{16,22},{18,... | collective-permute-start | bytes 1179656 | tf_op jit(solution)/shard_map/ppermute | solution.py:286
  212.3 11.9 %collective-permute-start.17 = (bf16[512,256]{1,0:T(8,128)(2,1)}, bf16[512,256]{1,0:T(8,128)(2,1)S(1)}, u32[]{:S(2)}, u32[]{:S(2)}) collective-permute-start(bf16[512,256]{1,0:T(8,128)(2,1)} %get-tuple-element.53), channel_id=1, source_target_pairs={{0,2},{2,0},{4,6},{6,4},{8,10},{10,8},{12,14},{14,12},{16,18},{18,... | collective-permute-start | bytes 786440 | tf_op jit(solution)/shard_map/ppermute | solution.py:286
  212.6 13.7 %collective-permute-start.19 = (bf16[512,256]{1,0:T(8,128)(2,1)}, bf16[512,256]{1,0:T(8,128)(2,1)S(1)}, u32[]{:S(2)}, u32[]{:S(2)}) collective-permute-start(bf16[512,256]{1,0:T(8,128)(2,1)} %get-tuple-element.54), channel_id=1, source_target_pairs={{0,4},{2,6},{4,0},{6,2},{8,12},{10,14},{12,8},{14,10},{16,20},{18,... | collective-permute-start | bytes 786440 | tf_op jit(solution)/shard_map/ppermute | solution.py:286
  212.6 11.6 %copy-start.6 = (bf16[512,384]{1,0:T(8,128)(2,1)}, bf16[512,384]{1,0:T(8,128)(2,1)S(1)}, u32[]{:S(2)}) copy-start(bf16[512,384]{1,0:T(8,128)(2,1)S(1)} %collective-permute-done.16.refs_2_) | copy-start | bytes 1179652
  212.6 13.7 %collective-permute-start.21 = (bf16[512,256]{1,0:T(8,128)(2,1)}, bf16[512,256]{1,0:T(8,128)(2,1)S(1)}, u32[]{:S(2)}, u32[]{:S(2)}) collective-permute-start(bf16[512,256]{1,0:T(8,128)(2,1)} %get-tuple-element.50), channel_id=1, source_target_pairs={{0,6},{2,4},{4,2},{6,0},{8,14},{10,12},{12,10},{14,8},{16,22},{18,... | collective-permute-start | bytes 786440 | tf_op jit(solution)/shard_map/ppermute | solution.py:286
  224.2 2.1 copy-start.5
  (4 other events, 4.6 us)
Sparse Core Ops, SparseCore 0:
  38.6 92.8 all-gather.2
  133.1 55.9 all-gather.4
where the time goes:
time: 241 us; the launch traced here: 238 us
  waiting for transfers between devices  84.6 us (35%)
  Pallas kernels  77.8 us (32%)
  starting transfers between devices  28 us (12%)
  local copies, waits for them, and re-layouts  20 us (8%)
  between operations  13.6 us (6%)
  other arithmetic  13.4 us (6%)
    pallas_call x4, Pallas kernels, attend(): pl.pallas_call(kernel, out_shape=[jax.ShapeDtypeStruct((rows, columns), j...  74.4 us
    ppermute x16, waiting for transfers between devices, swapped(): lax.ppermute(block, 'ctx', [(i, i ^ distance) for i in range(devices)])  38.8 us
    ppermute x1, waiting for transfers between devices, planar(): lax.ppermute(kv_own, 'ctx', [(i, i + group) for i in range(devices - grou...  36.4 us
    ppermute x16, starting transfers between devices, swapped(): lax.ppermute(block, 'ctx', [(i, i ^ distance) for i in range(devices)])  22.4 us
    slice x2, local copies, waits for them, and re-layouts, planar(): relay_y, relay_x = (from_y[:, :half], from_x[:, half:])  4.95 us
  transfers between devices with their start and end apart: 24, of which 10 were waited for; matrix products, arithmetic and copies ran while one was open for 11% of the time, Pallas kernels for 31%

commit v1 on v0

--- a/solution.py
+++ b/solution.py
@@ -299,8 +299,13 @@
     first_columns = (q_width // HD + 1) // 2 * HD
     cuts = ((0, first_columns), (first_columns, q_width))
 
-    w_cut = [columns_for(w_query, d, 0, q_width, q_width, 1) for d in range(group)]
-    w_plane = w_cut[:1] + [swapped(w_cut[d], d) for d in far]
+    def w_blocks_of(chunk, *earlier):
+        low, high = cuts[chunk]
+        blocks = after([columns_for(w_query, d, low, high - low, q_width, 1) for d in range(group)], *earlier)
+        return blocks[:1] + [swapped(blocks[d], d) for d in far]
+
+    w_first = w_blocks_of(0)
+
     float_tokens = tokens.astype(jnp.float32)
     squares = jnp.sum(float_tokens * float_tokens, axis=-1)
     squares = squares + other_core(squares)
@@ -308,8 +313,7 @@
     gain = lax.dynamic_slice_in_dim(norm_gain, core * width, width, 0)
     normed = (float_tokens * inverse[:, None] * gain).astype(jnp.bfloat16)
 
-    w_plane = after(w_plane, normed)
-    w_stacks = [jnp.stack([block[:, low:high] for block in w_plane]) for low, high in cuts]
+    w_stacks = [jnp.stack(after(w_first, normed))]
     w_chunks = [lax.all_gather(w_stacks[0], "ctx", axis=0, tiled=True, axis_index_groups=lines)]
 
     (keys_later,) = after([cache_keys], w_stacks[0])
@@ -325,7 +329,8 @@
         cut = [columns_for(array, d, 0, kv_width, kv_width, 2).reshape(-1, kv_width) for array in (kv_before, kv_own)]
         return jnp.concatenate(cut + [bytes_own])
 
-    kv_cut = after([kv_for(d) for d in range(group)], w_stacks[1])
+    kv_cut = [kv_for(d) for d in range(group)]
+    w_stacks.append(jnp.stack(w_blocks_of(1, *kv_cut)))
     kv_parts = kv_cut[:1] + [swapped(kv_cut[d], d) for d in far]
 
     sent = jnp.stack([part[4 * tok_rows :] for part in kv_parts]).astype(jnp.int32)
@@ -338,7 +343,7 @@
 
     half = width // 2
     relay_y, relay_x = from_y[:, :half], from_x[:, half:]
-    from_x, from_y, relay_y, relay_x = after([from_x, from_y, relay_y, relay_x], *kv_parts)
+    from_x, from_y, relay_y, relay_x = after([from_x, from_y, relay_y, relay_x], *kv_parts, w_stacks[1])
     corner_a, corner_b = swapped(relay_y, 1), swapped(relay_x, 2)
     token_parts = [[normed, mine_other]] + [[from_x, other_core(from_x)], [from_y, other_core(from_y)]]
 

time: 241 us -> 245 us (1.017)
  the two profiles are of different devices: /device:TPU:0 before, /device:TPU:10 now
where the time goes in v1:
time: 245 us; the launch traced here: 247 us
  waiting for transfers between devices  92.7 us (38%)
  Pallas kernels  83.9 us (34%)
  starting transfers between devices  27 us (11%)
  local copies, waits for them, and re-layouts  15.2 us (6%)
  other arithmetic  14.1 us (6%)
  between operations  13.7 us (6%)
    pallas_call x4, Pallas kernels, attend(): pl.pallas_call(kernel, out_shape=[jax.ShapeDtypeStruct((rows, columns), j...  80.5 us
    ppermute x1, waiting for transfers between devices, planar(): lax.ppermute(kv_own, 'ctx', [(i, i + group) for i in range(devices - grou...  64.1 us
    ppermute x19, waiting for transfers between devices, swapped(): lax.ppermute(block, 'ctx', [(i, i ^ distance) for i in range(devices)])  23.2 us
    ppermute x19, starting transfers between devices, swapped(): lax.ppermute(block, 'ctx', [(i, i ^ distance) for i in range(devices)])  22.7 us
    ppermute x5, waiting for transfers between devices, other_core(): return lax.ppermute(block, 'tp', [(0, 1), (1, 0)])  5.34 us
    slice x2, local copies, waits for them, and re-layouts, planar(): relay_y, relay_x = (from_y[:, :half], from_x[:, half:])  4.95 us
  transfers between devices with their start and end apart: 27, of which 12 were waited for; matrix products, arithmetic and copies ran while one was open for 10% of the time, Pallas kernels for 33%

profile of v1, /device:TPU:10, one launch (start us, length us, event | category | flops | bytes accessed | tf_op | source)
XLA Modules:
  0.0 246.6 jit_solution(345228235116434650)
XLA Ops:
  6.5 2.5 %fusion = f32[512]{0:T(512)S(1)} fusion(bf16[512,2560]{1,0:T(8,128)(2,1)} %param.7), kind=kLoop, calls=%fused_computation.2 | loop fusion | flops 3931648 | bytes 2623488 | tf_op jit(solution)/shard_map/reduce_sum | solution.py:310
  9.1 2.2 constant_dynamic-slice_fusion.8
  11.9 1.5 collective-permute-start.1
  13.4 1.4 collective-permute-start.2
  15.0 2.2 fusion.2.refs_7_.refs_3_
  17.1 3.3 %collective-permute-done = bf16[320,384]{1,0:T(8,128)(2,1)} collective-permute-done((bf16[320,384]{1,0:T(8,128)(2,1)}, bf16[320,384]{1,0:T(8,128)(2,1)}, u32[]{:S(2)}, u32[]{:S(2)}) %collective-permute-start) | collective-permute-done | bytes 245792 | tf_op jit(solution)/shard_map/ppermute | solution.py:286
  20.4 4.1 %collective-permute-done.1 = bf16[320,384]{1,0:T(8,128)(2,1)} collective-permute-done((bf16[320,384]{1,0:T(8,128)(2,1)}, bf16[320,384]{1,0:T(8,128)(2,1)}, u32[]{:S(2)}, u32[]{:S(2)}) %collective-permute-start.1) | collective-permute-done | bytes 245792 | tf_op jit(solution)/shard_map/ppermute | solution.py:286
  24.6 1.6 collective-permute-done.2
  26.2 2.3 pad_maximum_fusion.5
  29.5 1.5 collective-permute-start.8
  31.0 2.1 pad_maximum_fusion
  33.1 3.5 %collective-permute-start.4 = (bf16[2,512,512]{2,1,0:T(8,128)(2,1)}, bf16[2,512,512]{2,1,0:T(8,128)(2,1)}, u32[]{:S(2)}, u32[]{:S(2)}) collective-permute-start(bf16[2,512,512]{2,1,0:T(8,128)(2,1)} %pad_maximum_fusion), channel_id=1, source_target_pairs={{0,8},{2,10},{4,12},{6,14},{8,16},{10,18},{12,20},{14,22},{16,24},... | collective-permute-start | bytes 3145736 | tf_op jit(solution)/shard_map/ppermute | solution.py:321
  36.8 1.4 constant_dynamic-slice_fusion
  39.5 64.1 %collective-permute-done.4 = bf16[2,512,512]{2,1,0:T(8,128)(2,1)} collective-permute-done((bf16[2,512,512]{2,1,0:T(8,128)(2,1)}, bf16[2,512,512]{2,1,0:T(8,128)(2,1)}, u32[]{:S(2)}, u32[]{:S(2)}) %collective-permute-start.4) | collective-permute-done | bytes 1048608 | tf_op jit(solution)/shard_map/ppermute | solution.py:321
  104.9 1.4 pad_maximum_fusion.1
  106.3 2.2 collective-permute-start.11
  109.8 4.5 %collective-permute-done.12 = bf16[320,256]{1,0:T(8,128)(2,1)S(1)} collective-permute-done((bf16[320,256]{1,0:T(8,128)(2,1)S(1)}, bf16[320,256]{1,0:T(8,128)(2,1)S(1)}, u32[]{:S(2)}, u32[]{:S(2)}) %collective-permute-start.12) | collective-permute-done | bytes 163872 | tf_op jit(solution)/shard_map/ppermute | solution.py:286
  118.7 2.5 %slice.35 = bf16[512,1280]{1,0:T(8,128)(2,1)} slice(bf16[512,2560]{1,0:T(8,128)(2,1)} %collective-permute-done.9.refs_3_.refs_5_), slice={[0:512], [0:1280]} | slice | bytes 2621440 | tf_op jit(solution)/shard_map/slice | solution.py:345
  121.1 2.5 %slice.36 = bf16[512,1280]{1,0:T(8,128)(2,1)} slice(bf16[512,2560]{1,0:T(8,128)(2,1)} %collective-permute-done.8.refs_5_.refs_7_), slice={[0:512], [1280:2560]} | slice | bytes 2621440 | tf_op jit(solution)/shard_map/slice | solution.py:345
  124.7 5.7 %collective-permute-done.6.refs_12_.refs_8_ = bf16[2080,128]{1,0:T(8,128)(2,1)} collective-permute-done((bf16[2080,128]{1,0:T(8,128)(2,1)}, bf16[2080,128]{1,0:T(8,128)(2,1)}, u32[]{:S(2)}, u32[]{:S(2)}) %collective-permute-start.6) | collective-permute-done | bytes 532512 | tf_op jit(solution)/shard_map/ppermute | solution.py:286
  135.7 3.7 %collective-permute-done.14.refs_6_.refs_8_ = bf16[512,2560]{1,0:T(8,128)(2,1)} collective-permute-done((bf16[512,2560]{1,0:T(8,128)(2,1)}, bf16[512,2560]{1,0:T(8,128)(2,1)}, u32[]{:S(2)}, u32[]{:S(2)}) %collective-permute-start.14) | collective-permute-done | bytes 2621472 | tf_op jit(solution)/shard_map/ppermute | solution.py:289
  139.4 31.6 %shard_map.73 = (bf16[512,384]{1,0:T(8,128)(2,1)}, bf16[512,384]{1,0:T(8,128)(2,1)}, bf16[512,384]{1,0:T(8,128)(2,1)}) custom-call(s32[3]{0:T(128)} %pad_add_fusion.1.refs_0_.info_ref, s32[4,6,128]{2,1,0:T(8,128)} %fusion.8.refs_1_.refs_2_, s32[4,6,128]{2,1,0:T(8,128)} %fusion.8.refs_1_.refs_2_, bf16[512,2560]{1,0:T(8,128)(2,1)} %collective-permute-done.9.refs_3_.refs_5_, ...), custom_call_target="tpu_custom_call" | custom-call | flops 8455716864 | bytes 22937600 | tf_op jit(solution)/shard_map/pallas_call | solution.py:238
  171.1 1.4 constant_dynamic-update-slice_fusion.1
  172.5 1.4 constant_dynamic-update-slice_fusion.refs_3_
  174.2 3.9 %collective-permute-start.21 = (bf16[512,384]{1,0:T(8,128)(2,1)}, bf16[512,384]{1,0:T(8,128)(2,1)S(1)}, u32[]{:S(2)}, u32[]{:S(2)}) collective-permute-start(bf16[512,384]{1,0:T(8,128)(2,1)} %get-tuple-element.50), channel_id=1, source_target_pairs={{0,4},{2,6},{4,0},{6,2},{8,12},{10,14},{12,8},{14,10},{16,20},{18,... | collective-permute-start | bytes 1179656 | tf_op jit(solution)/shard_map/ppermute | solution.py:286
  179.1 14.8 %shard_map.74 = bf16[512,384]{1,0:T(8,128)(2,1)} custom-call(s32[3]{0:T(128)} %pad_add_fusion.1.refs_0_.info_ref, s32[4,6,128]{2,1,0:T(8,128)} %fusion.8.refs_1_.refs_2_, s32[4,6,128]{2,1,0:T(8,128)} %fusion.8.refs_1_.refs_2_, bf16[512,2560]{1,0:T(8,128)(2,1)} %copy-done.2, bf16[512,2560]{1,0:T(8,128)(2,1)} %collective-permute-done.18.refs_4_, ...), custom_call_target="tpu_custom_call" | custom-call | flops 2818572288 | bytes 11665408 | tf_op jit(solution)/shard_map/pallas_call | solution.py:238
  194.8 23.9 %shard_map.75 = (bf16[512,256]{1,0:T(8,128)(2,1)}, bf16[512,256]{1,0:T(8,128)(2,1)}, bf16[512,256]{1,0:T(8,128)(2,1)}) custom-call(s32[3]{0:T(128)} %pad_add_fusion.1.refs_0_.info_ref, s32[4,6,128]{2,1,0:T(8,128)} %fusion.8.refs_1_.refs_2_, s32[4,6,128]{2,1,0:T(8,128)} %fusion.8.refs_1_.refs_2_, bf16[512,2560]{1,0:T(8,128)(2,1)} %copy-done.2, ...), custom_call_target="tpu_custom_call" | custom-call | flops 5637144576 | bytes 21233664 | tf_op jit(solution)/shard_map/pallas_call | solution.py:238
  218.7 3.1 %collective-permute-start.20 = (bf16[512,256]{1,0:T(8,128)(2,1)}, bf16[512,256]{1,0:T(8,128)(2,1)S(1)}, u32[]{:S(2)}, u32[]{:S(2)}) collective-permute-start(bf16[512,256]{1,0:T(8,128)(2,1)} %get-tuple-element.61), channel_id=1, source_target_pairs={{0,2},{2,0},{4,6},{6,4},{8,10},{10,8},{12,14},{14,12},{16,18},{18,... | collective-permute-start | bytes 786440 | tf_op jit(solution)/shard_map/ppermute | solution.py:286
  221.8 1.5 collective-permute-start.24
  223.4 10.2 %shard_map.76.refs_1_ = bf16[512,256]{1,0:T(8,128)(2,1)} custom-call(s32[3]{0:T(128)} %pad_add_fusion.1.refs_0_.info_ref, s32[4,6,128]{2,1,0:T(8,128)} %fusion.8.refs_1_.refs_2_, s32[4,6,128]{2,1,0:T(8,128)} %fusion.8.refs_1_.refs_2_, bf16[512,2560]{1,0:T(8,128)(2,1)} %fusion.2.refs_7_.refs_3_, bf16[512,2560]{1,0:T(8,128)(2,1)} %collective-permute-done.15.refs_8_.refs_4_, ...), custom_call_target="tpu_custom_call" | custom-call | flops 1879048192 | bytes 10223616 | tf_op jit(solution)/shard_map/pallas_call | solution.py:238
  233.7 1.7 collective-permute-done.22.refs_5_
  236.3 3.4 %shard_map.77 = bf16[512,2560]{1,0:T(8,128)(2,1)} custom-call(s32[3]{0:T(128)} %pad_add_fusion.1.refs_0_.info_ref, bf16[512,384]{1,0:T(8,128)(2,1)} %get-tuple-element.49.refs_0_, bf16[512,256]{1,0:T(8,128)(2,1)} %shard_map.76.refs_1_, bf16[512,384]{1,0:T(8,128)(2,1)} %copy-done.6, bf16[512,256]{1,0:T(8,128)(2,1)} %copy-done.8, bf16[512,384]{1,0:T(8,128)(2,1)} %copy-done.5, ...), custom_call_target="tpu_custom_call" | custom-call | bytes 5242880 | tf_op jit(solution)/shard_map/pallas_call | solution.py:380
  (82 shorter events, 19.6 us)
Async XLA Ops:
  6.5 132.9 %all-gather.3.cloned.1.call-start = ((), (), s32[]{:S(2)}) async-start(), calls=%async_computation | async-start | bytes 4915200 | tf_op jit(solution)/shard_map/all_gather | solution.py:317
  9.0 5.9 %collective-permute-start.3 = (f32[512]{0:T(512)S(1)}, f32[512]{0:T(512)S(1)}, u32[]{:S(2)}, u32[]{:S(2)}) collective-permute-start(f32[512]{0:T(512)S(1)} %fusion), channel_id=1, source_target_pairs={{0,1},{1,0},{2,3},{3,2},{4,5},{5,4},{6,7},{7,6},{8,9},{9,8},{10,11... | collective-permute-start | bytes 6152 | tf_op jit(solution)/shard_map/ppermute | solution.py:289
  11.4 9.1 %collective-permute-start = (bf16[320,384]{1,0:T(8,128)(2,1)}, bf16[320,384]{1,0:T(8,128)(2,1)}, u32[]{:S(2)}, u32[]{:S(2)}) collective-permute-start(bf16[320,384]{1,0:T(8,128)(2,1)} %get-tuple-element.35), channel_id=1, source_target_pairs={{0,2},{2,0},{4,6},{6,4},{8,10},{10,8},{12,14},{14,12},{16,18},{18,... | collective-permute-start | bytes 737288 | tf_op jit(solution)/shard_map/ppermute | solution.py:286
  11.9 12.7 %collective-permute-start.1 = (bf16[320,384]{1,0:T(8,128)(2,1)}, bf16[320,384]{1,0:T(8,128)(2,1)}, u32[]{:S(2)}, u32[]{:S(2)}) collective-permute-start(bf16[320,384]{1,0:T(8,128)(2,1)} %get-tuple-element.36), channel_id=1, source_target_pairs={{0,4},{2,6},{4,0},{6,2},{8,12},{10,14},{12,8},{14,10},{16,20},{18,... | collective-permute-start | bytes 737288 | tf_op jit(solution)/shard_map/ppermute | solution.py:286
  13.4 12.8 %collective-permute-start.2 = (bf16[320,384]{1,0:T(8,128)(2,1)}, bf16[320,384]{1,0:T(8,128)(2,1)}, u32[]{:S(2)}, u32[]{:S(2)}) collective-permute-start(bf16[320,384]{1,0:T(8,128)(2,1)} %get-tuple-element.37), channel_id=1, source_target_pairs={{0,6},{2,4},{4,2},{6,0},{8,14},{10,12},{12,10},{14,8},{16,22},{18,... | collective-permute-start | bytes 737288 | tf_op jit(solution)/shard_map/ppermute | solution.py:286
  15.0 16.1 %copy-start.4 = (bf16[512,512]{1,0:T(8,128)(2,1)S(1)}, bf16[512,512]{1,0:T(8,128)(2,1)}, u32[]{:S(2)}) copy-start(bf16[512,512]{1,0:T(8,128)(2,1)} %param.10) | copy-start | bytes 1572868
  17.1 19.5 %copy-start.12 = (s32[4,64]{1,0:T(4,128)S(1)}, s32[4,64]{1,0:T(4,128)}, u32[]{:S(2)}) copy-start(s32[4,64]{1,0:T(4,128)} %param.13) | copy-start | bytes 3076
  17.1 19.6 %copy-start.13 = (s32[512]{0:T(512)S(1)}, s32[512]{0:T(512)}, u32[]{:S(2)}) copy-start(s32[512]{0:T(512)} %param.12) | copy-start | bytes 6148
  28.6 166.2 %all-gather.5.cloned.1.call-start = ((), (), s32[]{:S(2)}) async-start(), calls=%async_computation.1 | async-start | bytes 3276800 | tf_op jit(solution)/shard_map/all_gather | solution.py:342
  28.6 90.0 %collective-permute-start.9 = (bf16[512,2560]{1,0:T(8,128)(2,1)S(1)}, bf16[512,2560]{1,0:T(8,128)(2,1)}, u32[]{:S(2)}, u32[]{:S(2)}) collective-permute-start(bf16[512,2560]{1,0:T(8,128)(2,1)S(1)} %copy-done.1), channel_id=1, source_target_pairs={{0,4},{2,6},{4,0},{6,2},{8,12},{10,14},{12,8},{14,10},{16,20},{18,... | collective-permute-start | bytes 7864328 | tf_op jit(solution)/shard_map/ppermute | solution.py:286
  29.5 91.6 %collective-permute-start.8 = (bf16[512,2560]{1,0:T(8,128)(2,1)S(1)}, bf16[512,2560]{1,0:T(8,128)(2,1)}, u32[]{:S(2)}, u32[]{:S(2)}) collective-permute-start(bf16[512,2560]{1,0:T(8,128)(2,1)S(1)} %copy-done.1), channel_id=1, source_target_pairs={{0,2},{2,0},{4,6},{6,4},{8,10},{10,8},{12,14},{14,12},{16,18},{18,... | collective-permute-start | bytes 7864328 | tf_op jit(solution)/shard_map/ppermute | solution.py:286
  33.1 70.4 %collective-permute-start.4 = (bf16[2,512,512]{2,1,0:T(8,128)(2,1)}, bf16[2,512,512]{2,1,0:T(8,128)(2,1)}, u32[]{:S(2)}, u32[]{:S(2)}) collective-permute-start(bf16[2,512,512]{2,1,0:T(8,128)(2,1)} %pad_maximum_fusion), channel_id=1, source_target_pairs={{0,8},{2,10},{4,12},{6,14},{8,16},{10,18},{12,20},{14,22},{16,24},... | collective-permute-start | bytes 3145736 | tf_op jit(solution)/shard_map/ppermute | solution.py:321
  106.3 8.0 %collective-permute-start.12 = (bf16[320,256]{1,0:T(8,128)(2,1)S(1)}, bf16[320,256]{1,0:T(8,128)(2,1)S(1)}, u32[]{:S(2)}, u32[]{:S(2)}) collective-permute-start(bf16[320,256]{1,0:T(8,128)(2,1)S(1)} %get-tuple-element.46), channel_id=1, source_target_pairs={{0,6},{2,4},{4,2},{6,0},{8,14},{10,12},{12,10},{14,8},{16,22},{18,... | collective-permute-start | bytes 491528 | tf_op jit(solution)/shard_map/ppermute | solution.py:286
  106.3 9.1 %collective-permute-start.11 = (bf16[320,256]{1,0:T(8,128)(2,1)S(1)}, bf16[320,256]{1,0:T(8,128)(2,1)S(1)}, u32[]{:S(2)}, u32[]{:S(2)}) collective-permute-start(bf16[320,256]{1,0:T(8,128)(2,1)S(1)} %get-tuple-element.45), channel_id=1, source_target_pairs={{0,4},{2,6},{4,0},{6,2},{8,12},{10,14},{12,8},{14,10},{16,20},{18,... | collective-permute-start | bytes 491528 | tf_op jit(solution)/shard_map/ppermute | solution.py:286
  108.5 8.0 %collective-permute-start.10 = (bf16[320,256]{1,0:T(8,128)(2,1)S(1)}, bf16[320,256]{1,0:T(8,128)(2,1)S(1)}, u32[]{:S(2)}, u32[]{:S(2)}) collective-permute-start(bf16[320,256]{1,0:T(8,128)(2,1)S(1)} %get-tuple-element.44), channel_id=1, source_target_pairs={{0,2},{2,0},{4,6},{6,4},{8,10},{10,8},{12,14},{14,12},{16,18},{18,... | collective-permute-start | bytes 491528 | tf_op jit(solution)/shard_map/ppermute | solution.py:286
  114.2 10.5 %collective-permute-start.7 = (bf16[2080,128]{1,0:T(8,128)(2,1)}, bf16[2080,128]{1,0:T(8,128)(2,1)S(1)}, u32[]{:S(2)}, u32[]{:S(2)}) collective-permute-start(bf16[2080,128]{1,0:T(8,128)(2,1)} %get-tuple-element.81), channel_id=1, source_target_pairs={{0,6},{2,4},{4,2},{6,0},{8,14},{10,12},{12,10},{14,8},{16,22},{18,... | collective-permute-start | bytes 1597448 | tf_op jit(solution)/shard_map/ppermute | solution.py:286
  115.4 15.1 %collective-permute-start.6 = (bf16[2080,128]{1,0:T(8,128)(2,1)}, bf16[2080,128]{1,0:T(8,128)(2,1)}, u32[]{:S(2)}, u32[]{:S(2)}) collective-permute-start(bf16[2080,128]{1,0:T(8,128)(2,1)} %get-tuple-element.80), channel_id=1, source_target_pairs={{0,4},{2,6},{4,0},{6,2},{8,12},{10,14},{12,8},{14,10},{16,20},{18,... | collective-permute-start | bytes 1597448 | tf_op jit(solution)/shard_map/ppermute | solution.py:286
  116.5 13.9 %collective-permute-start.5 = (bf16[2080,128]{1,0:T(8,128)(2,1)}, bf16[2080,128]{1,0:T(8,128)(2,1)}, u32[]{:S(2)}, u32[]{:S(2)}) collective-permute-start(bf16[2080,128]{1,0:T(8,128)(2,1)} %get-tuple-element.82), channel_id=1, source_target_pairs={{0,2},{2,0},{4,6},{6,4},{8,10},{10,8},{12,14},{14,12},{16,18},{18,... | collective-permute-start | bytes 1597448 | tf_op jit(solution)/shard_map/ppermute | solution.py:286
  118.7 16.5 %collective-permute-start.15 = (bf16[512,2560]{1,0:T(8,128)(2,1)S(1)}, bf16[512,2560]{1,0:T(8,128)(2,1)}, u32[]{:S(2)}, u32[]{:S(2)}) collective-permute-start(bf16[512,2560]{1,0:T(8,128)(2,1)S(1)} %copy-done.1), channel_id=1, source_target_pairs={{0,1},{1,0},{2,3},{3,2},{4,5},{5,4},{6,7},{7,6},{8,9},{9,8},{10,11... | collective-permute-start | bytes 7864328 | tf_op jit(solution)/shard_map/ppermute | solution.py:289
  124.7 14.7 %copy-start.3 = (bf16[2080,128]{1,0:T(8,128)(2,1)}, bf16[2080,128]{1,0:T(8,128)(2,1)S(1)}, u32[]{:S(2)}) copy-start(bf16[2080,128]{1,0:T(8,128)(2,1)S(1)} %collective-permute-done.7.refs_13_.refs_9_) | copy-start | bytes 1597444
  130.4 5.3 %collective-permute-start.13 = (bf16[512,2560]{1,0:T(8,128)(2,1)}, bf16[512,2560]{1,0:T(8,128)(2,1)}, u32[]{:S(2)}, u32[]{:S(2)}) collective-permute-start(bf16[512,2560]{1,0:T(8,128)(2,1)} %collective-permute-done.9.refs_3_.refs_5_), channel_id=1, source_target_pairs={{0,1},{1,0},{2,3},{3,2},{4,5},{5,4},{6,7},{7,6},{8,9},{9,8},{10,11... | collective-permute-start | bytes 7864328 | tf_op jit(solution)/shard_map/ppermute | solution.py:289
  130.4 9.0 %collective-permute-start.14 = (bf16[512,2560]{1,0:T(8,128)(2,1)}, bf16[512,2560]{1,0:T(8,128)(2,1)}, u32[]{:S(2)}, u32[]{:S(2)}) collective-permute-start(bf16[512,2560]{1,0:T(8,128)(2,1)} %collective-permute-done.8.refs_5_.refs_7_), channel_id=1, source_target_pairs={{0,1},{1,0},{2,3},{3,2},{4,5},{5,4},{6,7},{7,6},{8,9},{9,8},{10,11... | collective-permute-start | bytes 7864328 | tf_op jit(solution)/shard_map/ppermute | solution.py:289
  131.7 39.4 %collective-permute-start.16 = (bf16[512,1280]{1,0:T(8,128)(2,1)}, bf16[512,1280]{1,0:T(8,128)(2,1)}, u32[]{:S(2)}, u32[]{:S(2)}) collective-permute-start(bf16[512,1280]{1,0:T(8,128)(2,1)} %slice.35), channel_id=1, source_target_pairs={{0,2},{2,0},{4,6},{6,4},{8,10},{10,8},{12,14},{14,12},{16,18},{18,... | collective-permute-start | bytes 3932168 | tf_op jit(solution)/shard_map/ppermute | solution.py:286
  132.5 38.6 %collective-permute-start.17 = (bf16[512,1280]{1,0:T(8,128)(2,1)}, bf16[512,1280]{1,0:T(8,128)(2,1)}, u32[]{:S(2)}, u32[]{:S(2)}) collective-permute-start(bf16[512,1280]{1,0:T(8,128)(2,1)} %slice.36), channel_id=1, source_target_pairs={{0,4},{2,6},{4,0},{6,2},{8,12},{10,14},{12,8},{14,10},{16,20},{18,... | collective-permute-start | bytes 3932168 | tf_op jit(solution)/shard_map/ppermute | solution.py:286
  174.0 5.1 %collective-permute-start.18 = (bf16[512,2560]{1,0:T(8,128)(2,1)S(1)}, bf16[512,2560]{1,0:T(8,128)(2,1)}, u32[]{:S(2)}, u32[]{:S(2)}) collective-permute-start(bf16[512,2560]{1,0:T(8,128)(2,1)S(1)} %constant_dynamic-update-slice_fusion.refs_3_), channel_id=1, source_target_pairs={{0,1},{1,0},{2,3},{3,2},{4,5},{5,4},{6,7},{7,6},{8,9},{9,8},{10,11... | collective-permute-start | bytes 7864328 | tf_op jit(solution)/shard_map/ppermute | solution.py:289
  174.2 59.5 %collective-permute-start.21 = (bf16[512,384]{1,0:T(8,128)(2,1)}, bf16[512,384]{1,0:T(8,128)(2,1)S(1)}, u32[]{:S(2)}, u32[]{:S(2)}) collective-permute-start(bf16[512,384]{1,0:T(8,128)(2,1)} %get-tuple-element.50), channel_id=1, source_target_pairs={{0,4},{2,6},{4,0},{6,2},{8,12},{10,14},{12,8},{14,10},{16,20},{18,... | collective-permute-start | bytes 1179656 | tf_op jit(solution)/shard_map/ppermute | solution.py:286
  178.0 43.8 %collective-permute-start.19 = (bf16[512,384]{1,0:T(8,128)(2,1)}, bf16[512,384]{1,0:T(8,128)(2,1)S(1)}, u32[]{:S(2)}, u32[]{:S(2)}) collective-permute-start(bf16[512,384]{1,0:T(8,128)(2,1)} %get-tuple-element.60), channel_id=1, source_target_pairs={{0,2},{2,0},{4,6},{6,4},{8,10},{10,8},{12,14},{14,12},{16,18},{18,... | collective-permute-start | bytes 1179656 | tf_op jit(solution)/shard_map/ppermute | solution.py:286
  193.8 41.5 %collective-permute-start.23 = (bf16[512,384]{1,0:T(8,128)(2,1)}, bf16[512,384]{1,0:T(8,128)(2,1)S(1)}, u32[]{:S(2)}, u32[]{:S(2)}) collective-permute-start(bf16[512,384]{1,0:T(8,128)(2,1)} %shard_map.74), channel_id=1, source_target_pairs={{0,6},{2,4},{4,2},{6,0},{8,14},{10,12},{12,10},{14,8},{16,22},{18,... | collective-permute-start | bytes 1179656 | tf_op jit(solution)/shard_map/ppermute | solution.py:286
  218.7 14.9 %collective-permute-start.20 = (bf16[512,256]{1,0:T(8,128)(2,1)}, bf16[512,256]{1,0:T(8,128)(2,1)S(1)}, u32[]{:S(2)}, u32[]{:S(2)}) collective-permute-start(bf16[512,256]{1,0:T(8,128)(2,1)} %get-tuple-element.61), channel_id=1, source_target_pairs={{0,2},{2,0},{4,6},{6,4},{8,10},{10,8},{12,14},{14,12},{16,18},{18,... | collective-permute-start | bytes 786440 | tf_op jit(solution)/shard_map/ppermute | solution.py:286
  221.8 13.6 %collective-permute-start.22 = (bf16[512,256]{1,0:T(8,128)(2,1)}, bf16[512,256]{1,0:T(8,128)(2,1)S(1)}, u32[]{:S(2)}, u32[]{:S(2)}) collective-permute-start(bf16[512,256]{1,0:T(8,128)(2,1)} %get-tuple-element.62), channel_id=1, source_target_pairs={{0,4},{2,6},{4,0},{6,2},{8,12},{10,14},{12,8},{14,10},{16,20},{18,... | collective-permute-start | bytes 786440 | tf_op jit(solution)/shard_map/ppermute | solution.py:286
  221.8 11.8 %copy-start.6 = (bf16[512,384]{1,0:T(8,128)(2,1)}, bf16[512,384]{1,0:T(8,128)(2,1)S(1)}, u32[]{:S(2)}) copy-start(bf16[512,384]{1,0:T(8,128)(2,1)S(1)} %collective-permute-done.19.refs_2_) | copy-start | bytes 1179652
  221.8 13.6 %collective-permute-start.24 = (bf16[512,256]{1,0:T(8,128)(2,1)}, bf16[512,256]{1,0:T(8,128)(2,1)S(1)}, u32[]{:S(2)}, u32[]{:S(2)}) collective-permute-start(bf16[512,256]{1,0:T(8,128)(2,1)} %get-tuple-element.58), channel_id=1, source_target_pairs={{0,6},{2,4},{4,2},{6,0},{8,14},{10,12},{12,10},{14,8},{16,22},{18,... | collective-permute-start | bytes 786440 | tf_op jit(solution)/shard_map/ppermute | solution.py:286
  (9 other events, 39.3 us)
Sparse Core Ops, SparseCore 0:
  28.7 94.2 all-gather.2
  131.8 54.4 all-gather.4

commit v2 on v0

--- a/solution.py
+++ b/solution.py
@@ -300,6 +300,8 @@
     cuts = ((0, first_columns), (first_columns, q_width))
 
     w_cut = [columns_for(w_query, d, 0, q_width, q_width, 1) for d in range(group)]
+    kv_own = jnp.stack(after([cache_keys, cache_values], *w_cut))
+    kv_before = lax.ppermute(kv_own, "ctx", [(i, i + group) for i in range(devices - group)])
     w_plane = w_cut[:1] + [swapped(w_cut[d], d) for d in far]
     float_tokens = tokens.astype(jnp.float32)
     squares = jnp.sum(float_tokens * float_tokens, axis=-1)
@@ -308,13 +310,9 @@
     gain = lax.dynamic_slice_in_dim(norm_gain, core * width, width, 0)
     normed = (float_tokens * inverse[:, None] * gain).astype(jnp.bfloat16)
 
-    w_plane = after(w_plane, normed)
+    w_plane = after(w_plane, kv_before, normed)
     w_stacks = [jnp.stack([block[:, low:high] for block in w_plane]) for low, high in cuts]
     w_chunks = [lax.all_gather(w_stacks[0], "ctx", axis=0, tiled=True, axis_index_groups=lines)]
-
-    (keys_later,) = after([cache_keys], w_stacks[0])
-    kv_own = jnp.stack([keys_later, cache_values])
-    kv_before = lax.ppermute(kv_own, "ctx", [(i, i + group) for i in range(devices - group)])
 
     marks_own = marks_of(doc_start, tile_mask)
     marks_rows = marks_own.shape[0]

time: 241 us -> 243 us (level)
    ppermute x16, waiting for transfers between devices: 38.8 us -> 70.5 us  [swapped(): lax.ppermute(block, 'ctx', [(i, i ^ distance) for i in range(devices)])]
    ppermute x1, waiting for transfers between devices: 36.4 us -> 11.1 us  [planar(): lax.ppermute(kv_own, 'ctx', [(i, i + group) for i in range(devices - grou...]
    all_gather x1, waiting for transfers between devices: 4.66 us -> 0.02 us  [planar(): lax.all_gather(w_after, 'ctx', axis=0, tiled=True, axis_index_groups=lines)]
  transfers between devices with their start and end apart: 24 -> 24, of which waited for: 10 -> 8; matrix products, arithmetic and copies ran while one was open for 11% -> 11% of each run, Pallas kernels for 31% -> 31%
where the time goes in v2:
time: 243 us; the launch traced here: 240 us
  waiting for transfers between devices  84.8 us (35%)
  Pallas kernels  78 us (32%)
  starting transfers between devices  29.4 us (12%)
  local copies, waits for them, and re-layouts  21.2 us (9%)
  between operations  13.7 us (6%)
  other arithmetic  13.2 us (5%)
    pallas_call x4, Pallas kernels, attend(): pl.pallas_call(kernel, out_shape=[jax.ShapeDtypeStruct((rows, columns), j...  74.6 us
    ppermute x16, waiting for transfers between devices, swapped(): lax.ppermute(block, 'ctx', [(i, i ^ distance) for i in range(devices)])  70.5 us
    ppermute x16, starting transfers between devices, swapped(): lax.ppermute(block, 'ctx', [(i, i ^ distance) for i in range(devices)])  23.7 us
    ppermute x1, waiting for transfers between devices, planar(): lax.ppermute(kv_own, 'ctx', [(i, i + group) for i in range(devices - grou...  11.1 us
    ppermute x1, starting transfers between devices, planar(): lax.ppermute(kv_own, 'ctx', [(i, i + group) for i in range(devices - grou...  4.95 us
    slice x2, local copies, waits for them, and re-layouts, planar(): relay_y, relay_x = (from_y[:, :half], from_x[:, half:])  4.94 us
  transfers between devices with their start and end apart: 24, of which 8 were waited for; matrix products, arithmetic and copies ran while one was open for 11% of the time, Pallas kernels for 31%

profile of v2, /device:TPU:0, one launch (start us, length us, event | category | flops | bytes accessed | tf_op | source)
XLA Modules:
  0.0 240.2 jit_solution(16342586805428698812)
XLA Ops:
  6.5 2.7 %constant_dynamic-slice_fusion.4 = (bf16[320,640]{1,0:T(8,128)(2,1)}, bf16[320,640]{1,0:T(8,128)(2,1)}, bf16[320,640]{1,0:T(8,128)(2,1)S(1)}, bf16[320,640]{1,0:T(8,128)(2,1)}) fusion(bf16[320,2560]{1,0:T(8,128)(2,1)} %param.9, s32[]{:T(128)S(6)} %select_n.40, s32[]{:T(128)S(6)} %select_n.38, s32[]{:T(128)S(6)} %select_n.37, s32[]{:T(128)S(6)} %select_n.39), kind=kLoop, calls=%fused_computation.59 | loop fusion | bytes 3276816 | tf_op jit(solution)/shard_map/dynamic_slice | solution.py:293
  9.2 2.9 %collective-permute-start.1 = (bf16[320,640]{1,0:T(8,128)(2,1)}, bf16[320,640]{1,0:T(8,128)(2,1)}, u32[]{:S(2)}, u32[]{:S(2)}) collective-permute-start(bf16[320,640]{1,0:T(8,128)(2,1)} %get-tuple-element.58), channel_id=1, source_target_pairs={{0,2},{2,0},{4,6},{6,4},{8,10},{10,8},{12,14},{14,12},{16,18},{18,... | collective-permute-start | bytes 1228808 | tf_op jit(solution)/shard_map/ppermute | solution.py:286
  12.1 1.5 collective-permute-start.2
  15.9 5.0 %collective-permute-start = (bf16[2,512,512]{2,1,0:T(8,128)(2,1)}, bf16[2,512,512]{2,1,0:T(8,128)(2,1)}, u32[]{:S(2)}, u32[]{:S(2)}) collective-permute-start(bf16[2,512,512]{2,1,0:T(8,128)(2,1)} %pad_maximum_fusion), channel_id=1, source_target_pairs={{0,8},{2,10},{4,12},{6,14},{8,16},{10,18},{12,20},{14,22},{16,24},... | collective-permute-start | bytes 3145736 | tf_op jit(solution)/shard_map/ppermute | solution.py:304
  22.4 2.2 fusion.2.refs_7_.refs_3_
  24.5 7.6 %collective-permute-done.2 = bf16[320,640]{1,0:T(8,128)(2,1)} collective-permute-done((bf16[320,640]{1,0:T(8,128)(2,1)}, bf16[320,640]{1,0:T(8,128)(2,1)}, u32[]{:S(2)}, u32[]{:S(2)}) %collective-permute-start.2) | collective-permute-done | bytes 409632 | tf_op jit(solution)/shard_map/ppermute | solution.py:286
  32.2 11.1 %collective-permute-done = bf16[2,512,512]{2,1,0:T(8,128)(2,1)} collective-permute-done((bf16[2,512,512]{2,1,0:T(8,128)(2,1)}, bf16[2,512,512]{2,1,0:T(8,128)(2,1)}, u32[]{:S(2)}, u32[]{:S(2)}) %collective-permute-start) | collective-permute-done | bytes 1048608 | tf_op jit(solution)/shard_map/ppermute | solution.py:304
  46.6 1.6 collective-permute-start.9
  48.2 1.5 collective-permute-start.8
  49.7 1.3 reshape.35
  52.3 2.2 fusion.6
  57.5 1.4 constant_dynamic-slice_fusion
  60.7 1.6 collective-permute-start.6
  62.3 1.4 collective-permute-start.5
  63.7 44.5 %collective-permute-done.9.refs_3_.refs_5_ = bf16[512,2560]{1,0:T(8,128)(2,1)} collective-permute-done((bf16[512,2560]{1,0:T(8,128)(2,1)S(1)}, bf16[512,2560]{1,0:T(8,128)(2,1)}, u32[]{:S(2)}, u32[]{:S(2)}) %collective-permute-start.9) | collective-permute-done | bytes 2621472 | tf_op jit(solution)/shard_map/ppermute | solution.py:286
  108.2 2.5 %slice.71 = bf16[512,1280]{1,0:T(8,128)(2,1)} slice(bf16[512,2560]{1,0:T(8,128)(2,1)} %collective-permute-done.9.refs_3_.refs_5_), slice={[0:512], [0:1280]} | slice | bytes 2621440 | tf_op jit(solution)/shard_map/slice | solution.py:338
  110.6 2.5 %slice.72 = bf16[512,1280]{1,0:T(8,128)(2,1)} slice(bf16[512,2560]{1,0:T(8,128)(2,1)} %collective-permute-done.8.refs_5_.refs_7_), slice={[0:512], [1280:2560]} | slice | bytes 2621440 | tf_op jit(solution)/shard_map/slice | solution.py:338
  113.1 6.4 %collective-permute-done.7.refs_13_.refs_9_ = bf16[2080,128]{1,0:T(8,128)(2,1)} collective-permute-done((bf16[2080,128]{1,0:T(8,128)(2,1)S(1)}, bf16[2080,128]{1,0:T(8,128)(2,1)}, u32[]{:S(2)}, u32[]{:S(2)}) %collective-permute-start.7) | collective-permute-done | bytes 532512 | tf_op jit(solution)/shard_map/ppermute | solution.py:286
  119.5 8.6 %collective-permute-done.6.refs_12_.refs_8_ = bf16[2080,128]{1,0:T(8,128)(2,1)} collective-permute-done((bf16[2080,128]{1,0:T(8,128)(2,1)S(1)}, bf16[2080,128]{1,0:T(8,128)(2,1)}, u32[]{:S(2)}, u32[]{:S(2)}) %collective-permute-start.6) | collective-permute-done | bytes 532512 | tf_op jit(solution)/shard_map/ppermute | solution.py:286
  131.3 1.5 collective-permute-start.13
  135.3 3.1 %collective-permute-done.11.refs_6_.refs_8_ = bf16[512,2560]{1,0:T(8,128)(2,1)} collective-permute-done((bf16[512,2560]{1,0:T(8,128)(2,1)}, bf16[512,2560]{1,0:T(8,128)(2,1)}, u32[]{:S(2)}, u32[]{:S(2)}) %collective-permute-start.11) | collective-permute-done | bytes 2621472 | tf_op jit(solution)/shard_map/ppermute | solution.py:289
  138.4 27.5 %shard_map.73 = (bf16[512,384]{1,0:T(8,128)(2,1)}, bf16[512,384]{1,0:T(8,128)(2,1)}, bf16[512,384]{1,0:T(8,128)(2,1)}) custom-call(s32[3]{0:T(128)} %pad_add_fusion.1.refs_0_.info_ref, s32[4,6,128]{2,1,0:T(8,128)} %fusion.8.refs_1_.refs_2_, s32[4,6,128]{2,1,0:T(8,128)} %fusion.8.refs_1_.refs_2_, bf16[512,2560]{1,0:T(8,128)(2,1)} %collective-permute-done.9.refs_3_.refs_5_, ...), custom_call_target="tpu_custom_call" | custom-call | flops 8455716864 | bytes 22937600 | tf_op jit(solution)/shard_map/pallas_call | solution.py:238
  165.9 1.5 constant_dynamic-update-slice_fusion.1
  167.4 1.4 constant_dynamic-update-slice_fusion.refs_3_
  169.1 3.9 %collective-permute-start.18 = (bf16[512,384]{1,0:T(8,128)(2,1)S(1)}, bf16[512,384]{1,0:T(8,128)(2,1)S(1)}, u32[]{:S(2)}, u32[]{:S(2)}) collective-permute-start(bf16[512,384]{1,0:T(8,128)(2,1)S(1)} %copy-done.14), channel_id=1, source_target_pairs={{0,4},{2,6},{4,0},{6,2},{8,12},{10,14},{12,8},{14,10},{16,20},{18,... | collective-permute-start | bytes 1179656 | tf_op jit(solution)/shard_map/ppermute | solution.py:286
  173.0 3.1 %collective-permute-start.16 = (bf16[512,384]{1,0:T(8,128)(2,1)}, bf16[512,384]{1,0:T(8,128)(2,1)S(1)}, u32[]{:S(2)}, u32[]{:S(2)}) collective-permute-start(bf16[512,384]{1,0:T(8,128)(2,1)} %get-tuple-element.54), channel_id=1, source_target_pairs={{0,2},{2,0},{4,6},{6,4},{8,10},{10,8},{12,14},{14,12},{16,18},{18,... | collective-permute-start | bytes 1179656 | tf_op jit(solution)/shard_map/ppermute | solution.py:286
  176.1 15.5 %shard_map.74 = bf16[512,384]{1,0:T(8,128)(2,1)} custom-call(s32[3]{0:T(128)} %pad_add_fusion.1.refs_0_.info_ref, s32[4,6,128]{2,1,0:T(8,128)} %fusion.8.refs_1_.refs_2_, s32[4,6,128]{2,1,0:T(8,128)} %fusion.8.refs_1_.refs_2_, bf16[512,2560]{1,0:T(8,128)(2,1)} %copy-done.2, bf16[512,2560]{1,0:T(8,128)(2,1)} %collective-permute-done.15.refs_4_, ...), custom_call_target="tpu_custom_call" | custom-call | flops 2818572288 | bytes 11665408 | tf_op jit(solution)/shard_map/pallas_call | solution.py:238
  191.7 23.3 %shard_map.75 = (bf16[512,256]{1,0:T(8,128)(2,1)}, bf16[512,256]{1,0:T(8,128)(2,1)}, bf16[512,256]{1,0:T(8,128)(2,1)}) custom-call(s32[3]{0:T(128)} %pad_add_fusion.1.refs_0_.info_ref, s32[4,6,128]{2,1,0:T(8,128)} %fusion.8.refs_1_.refs_2_, s32[4,6,128]{2,1,0:T(8,128)} %fusion.8.refs_1_.refs_2_, bf16[512,2560]{1,0:T(8,128)(2,1)} %copy-done.2, ...), custom_call_target="tpu_custom_call" | custom-call | flops 5637144576 | bytes 21233664 | tf_op jit(solution)/shard_map/pallas_call | solution.py:238
  215.1 3.4 %collective-permute-start.21 = (bf16[512,256]{1,0:T(8,128)(2,1)}, bf16[512,256]{1,0:T(8,128)(2,1)S(1)}, u32[]{:S(2)}, u32[]{:S(2)}) collective-permute-start(bf16[512,256]{1,0:T(8,128)(2,1)} %get-tuple-element.52), channel_id=1, source_target_pairs={{0,6},{2,4},{4,2},{6,0},{8,14},{10,12},{12,10},{14,8},{16,22},{18,... | collective-permute-start | bytes 786440 | tf_op jit(solution)/shard_map/ppermute | solution.py:286
  218.5 8.3 %shard_map.76.refs_1_ = bf16[512,256]{1,0:T(8,128)(2,1)} custom-call(s32[3]{0:T(128)} %pad_add_fusion.1.refs_0_.info_ref, s32[4,6,128]{2,1,0:T(8,128)} %fusion.8.refs_1_.refs_2_, s32[4,6,128]{2,1,0:T(8,128)} %fusion.8.refs_1_.refs_2_, bf16[512,2560]{1,0:T(8,128)(2,1)} %fusion.2.refs_7_.refs_3_, bf16[512,2560]{1,0:T(8,128)(2,1)} %collective-permute-done.12.refs_8_.refs_4_, ...), custom_call_target="tpu_custom_call" | custom-call | flops 1879048192 | bytes 10223616 | tf_op jit(solution)/shard_map/pallas_call | solution.py:238
  226.9 2.1 collective-permute-done.19.refs_5_
  230.0 3.4 %shard_map.77 = bf16[512,2560]{1,0:T(8,128)(2,1)} custom-call(s32[3]{0:T(128)} %pad_add_fusion.1.refs_0_.info_ref, bf16[512,384]{1,0:T(8,128)(2,1)} %get-tuple-element.43.refs_0_, bf16[512,256]{1,0:T(8,128)(2,1)} %shard_map.76.refs_1_, bf16[512,384]{1,0:T(8,128)(2,1)} %copy-done.8, bf16[512,256]{1,0:T(8,128)(2,1)} %copy-done.10, bf16[512,384]{1,0:T(8,128)(2,1)} %copy-done.7, ...), custom_call_target="tpu_custom_call" | custom-call | bytes 5242880 | tf_op jit(solution)/shard_map/pallas_call | solution.py:373
  (81 shorter events, 20.3 us)
Async XLA Ops:
  6.5 7.1 %copy-start = (bf16[512,2560]{1,0:T(8,128)(2,1)S(1)}, bf16[512,2560]{1,0:T(8,128)(2,1)}, u32[]{:S(2)}) copy-start(bf16[512,2560]{1,0:T(8,128)(2,1)} %param.7) | copy-start | bytes 7864324
  6.5 131.9 %all-gather.3.cloned.1.call-start = ((), (), s32[]{:S(2)}) async-start(), calls=%async_computation | async-start | bytes 4915200 | tf_op jit(solution)/shard_map/all_gather | solution.py:315
  6.5 8.3 %copy-start.4 = (bf16[512,512]{1,0:T(8,128)(2,1)S(1)}, bf16[512,512]{1,0:T(8,128)(2,1)}, u32[]{:S(2)}) copy-start(bf16[512,512]{1,0:T(8,128)(2,1)} %param.10) | copy-start | bytes 1572868
  6.5 8.3 %copy-start.5 = (bf16[512,512]{1,0:T(8,128)(2,1)S(1)}, bf16[512,512]{1,0:T(8,128)(2,1)}, u32[]{:S(2)}) copy-start(bf16[512,512]{1,0:T(8,128)(2,1)} %param.11) | copy-start | bytes 1572868
  9.2 15.3 %collective-permute-start.1 = (bf16[320,640]{1,0:T(8,128)(2,1)}, bf16[320,640]{1,0:T(8,128)(2,1)}, u32[]{:S(2)}, u32[]{:S(2)}) collective-permute-start(bf16[320,640]{1,0:T(8,128)(2,1)} %get-tuple-element.58), channel_id=1, source_target_pairs={{0,2},{2,0},{4,6},{6,4},{8,10},{10,8},{12,14},{14,12},{16,18},{18,... | collective-permute-start | bytes 1228808 | tf_op jit(solution)/shard_map/ppermute | solution.py:286
  12.1 20.0 %collective-permute-start.2 = (bf16[320,640]{1,0:T(8,128)(2,1)}, bf16[320,640]{1,0:T(8,128)(2,1)}, u32[]{:S(2)}, u32[]{:S(2)}) collective-permute-start(bf16[320,640]{1,0:T(8,128)(2,1)} %get-tuple-element.60), channel_id=1, source_target_pairs={{0,4},{2,6},{4,0},{6,2},{8,12},{10,14},{12,8},{14,10},{16,20},{18,... | collective-permute-start | bytes 1228808 | tf_op jit(solution)/shard_map/ppermute | solution.py:286
  13.7 18.5 %collective-permute-start.3 = (bf16[320,640]{1,0:T(8,128)(2,1)}, bf16[320,640]{1,0:T(8,128)(2,1)}, u32[]{:S(2)}, u32[]{:S(2)}) collective-permute-start(bf16[320,640]{1,0:T(8,128)(2,1)} %get-tuple-element.57), channel_id=1, source_target_pairs={{0,6},{2,4},{4,2},{6,0},{8,14},{10,12},{12,10},{14,8},{16,22},{18,... | collective-permute-start | bytes 1228808 | tf_op jit(solution)/shard_map/ppermute | solution.py:286
  14.8 6.8 %collective-permute-start.4 = (f32[512]{0:T(512)}, f32[512]{0:T(512)}, u32[]{:S(2)}, u32[]{:S(2)}) collective-permute-start(f32[512]{0:T(512)} %fusion), channel_id=1, source_target_pairs={{0,1},{1,0},{2,3},{3,2},{4,5},{5,4},{6,7},{7,6},{8,9},{9,8},{10,11... | collective-permute-start | bytes 6152 | tf_op jit(solution)/shard_map/ppermute | solution.py:289
  15.9 27.3 %collective-permute-start = (bf16[2,512,512]{2,1,0:T(8,128)(2,1)}, bf16[2,512,512]{2,1,0:T(8,128)(2,1)}, u32[]{:S(2)}, u32[]{:S(2)}) collective-permute-start(bf16[2,512,512]{2,1,0:T(8,128)(2,1)} %pad_maximum_fusion), channel_id=1, source_target_pairs={{0,8},{2,10},{4,12},{6,14},{8,16},{10,18},{12,20},{14,22},{16,24},... | collective-permute-start | bytes 3145736 | tf_op jit(solution)/shard_map/ppermute | solution.py:304
  24.5 22.1 %copy-start.1 = (bf16[512,2560]{1,0:T(8,128)(2,1)S(1)}, bf16[512,2560]{1,0:T(8,128)(2,1)}, u32[]{:S(2)}) copy-start(bf16[512,2560]{1,0:T(8,128)(2,1)} %fusion.2.refs_7_.refs_3_) | copy-start | bytes 7864324
  46.6 145.1 %all-gather.5.cloned.1.call-start = ((), (), s32[]{:S(2)}) async-start(), calls=%async_computation.1 | async-start | bytes 3276800 | tf_op jit(solution)/shard_map/all_gather | solution.py:335
  46.6 61.5 %collective-permute-start.9 = (bf16[512,2560]{1,0:T(8,128)(2,1)S(1)}, bf16[512,2560]{1,0:T(8,128)(2,1)}, u32[]{:S(2)}, u32[]{:S(2)}) collective-permute-start(bf16[512,2560]{1,0:T(8,128)(2,1)S(1)} %copy-done.1), channel_id=1, source_target_pairs={{0,4},{2,6},{4,0},{6,2},{8,12},{10,14},{12,8},{14,10},{16,20},{18,... | collective-permute-start | bytes 7864328 | tf_op jit(solution)/shard_map/ppermute | solution.py:286
  48.2 62.4 %collective-permute-start.8 = (bf16[512,2560]{1,0:T(8,128)(2,1)S(1)}, bf16[512,2560]{1,0:T(8,128)(2,1)}, u32[]{:S(2)}, u32[]{:S(2)}) collective-permute-start(bf16[512,2560]{1,0:T(8,128)(2,1)S(1)} %copy-done.1), channel_id=1, source_target_pairs={{0,2},{2,0},{4,6},{6,4},{8,10},{10,8},{12,14},{14,12},{16,18},{18,... | collective-permute-start | bytes 7864328 | tf_op jit(solution)/shard_map/ppermute | solution.py:286
  54.5 4.4 %copy-start.13 = (bf16[32,128]{1,0:T(8,128)(2,1)S(1)}, bf16[32,128]{1,0:T(8,128)(2,1)}, u32[]{:S(2)}) copy-start(bf16[32,128]{1,0:T(8,128)(2,1)} %fusion.13) | copy-start | bytes 24580
  60.1 70.4 %copy-start.3 = (bf16[2080,128]{1,0:T(8,128)(2,1)}, bf16[2080,128]{1,0:T(8,128)(2,1)S(1)}, u32[]{:S(2)}) copy-start(bf16[2080,128]{1,0:T(8,128)(2,1)S(1)} %get-tuple-element.37.refs_10_.refs_6_) | copy-start | bytes 1597444
  60.1 59.4 %collective-permute-start.7 = (bf16[2080,128]{1,0:T(8,128)(2,1)S(1)}, bf16[2080,128]{1,0:T(8,128)(2,1)}, u32[]{:S(2)}, u32[]{:S(2)}) collective-permute-start(bf16[2080,128]{1,0:T(8,128)(2,1)S(1)} %get-tuple-element.40), channel_id=1, source_target_pairs={{0,6},{2,4},{4,2},{6,0},{8,14},{10,12},{12,10},{14,8},{16,22},{18,... | collective-permute-start | bytes 1597448 | tf_op jit(solution)/shard_map/ppermute | solution.py:286
  60.7 67.4 %collective-permute-start.6 = (bf16[2080,128]{1,0:T(8,128)(2,1)S(1)}, bf16[2080,128]{1,0:T(8,128)(2,1)}, u32[]{:S(2)}, u32[]{:S(2)}) collective-permute-start(bf16[2080,128]{1,0:T(8,128)(2,1)S(1)} %get-tuple-element.39), channel_id=1, source_target_pairs={{0,4},{2,6},{4,0},{6,2},{8,12},{10,14},{12,8},{14,10},{16,20},{18,... | collective-permute-start | bytes 1597448 | tf_op jit(solution)/shard_map/ppermute | solution.py:286
  62.3 67.1 %collective-permute-start.5 = (bf16[2080,128]{1,0:T(8,128)(2,1)S(1)}, bf16[2080,128]{1,0:T(8,128)(2,1)}, u32[]{:S(2)}, u32[]{:S(2)}) collective-permute-start(bf16[2080,128]{1,0:T(8,128)(2,1)S(1)} %get-tuple-element.38), channel_id=1, source_target_pairs={{0,2},{2,0},{4,6},{6,4},{8,10},{10,8},{12,14},{14,12},{16,18},{18,... | collective-permute-start | bytes 1597448 | tf_op jit(solution)/shard_map/ppermute | solution.py:286
  108.2 27.2 %collective-permute-start.12 = (bf16[512,2560]{1,0:T(8,128)(2,1)S(1)}, bf16[512,2560]{1,0:T(8,128)(2,1)}, u32[]{:S(2)}, u32[]{:S(2)}) collective-permute-start(bf16[512,2560]{1,0:T(8,128)(2,1)S(1)} %copy-done.1), channel_id=1, source_target_pairs={{0,1},{1,0},{2,3},{3,2},{4,5},{5,4},{6,7},{7,6},{8,9},{9,8},{10,11... | collective-permute-start | bytes 7864328 | tf_op jit(solution)/shard_map/ppermute | solution.py:289
  129.4 5.9 %collective-permute-start.10 = (bf16[512,2560]{1,0:T(8,128)(2,1)}, bf16[512,2560]{1,0:T(8,128)(2,1)}, u32[]{:S(2)}, u32[]{:S(2)}) collective-permute-start(bf16[512,2560]{1,0:T(8,128)(2,1)} %collective-permute-done.9.refs_3_.refs_5_), channel_id=1, source_target_pairs={{0,1},{1,0},{2,3},{3,2},{4,5},{5,4},{6,7},{7,6},{8,9},{9,8},{10,11... | collective-permute-start | bytes 7864328 | tf_op jit(solution)/shard_map/ppermute | solution.py:289
  129.4 9.0 %collective-permute-start.11 = (bf16[512,2560]{1,0:T(8,128)(2,1)}, bf16[512,2560]{1,0:T(8,128)(2,1)}, u32[]{:S(2)}, u32[]{:S(2)}) collective-permute-start(bf16[512,2560]{1,0:T(8,128)(2,1)} %collective-permute-done.8.refs_5_.refs_7_), channel_id=1, source_target_pairs={{0,1},{1,0},{2,3},{3,2},{4,5},{5,4},{6,7},{7,6},{8,9},{9,8},{10,11... | collective-permute-start | bytes 7864328 | tf_op jit(solution)/shard_map/ppermute | solution.py:289
  131.3 34.6 %collective-permute-start.13 = (bf16[512,1280]{1,0:T(8,128)(2,1)}, bf16[512,1280]{1,0:T(8,128)(2,1)}, u32[]{:S(2)}, u32[]{:S(2)}) collective-permute-start(bf16[512,1280]{1,0:T(8,128)(2,1)} %slice.71), channel_id=1, source_target_pairs={{0,2},{2,0},{4,6},{6,4},{8,10},{10,8},{12,14},{14,12},{16,18},{18,... | collective-permute-start | bytes 3932168 | tf_op jit(solution)/shard_map/ppermute | solution.py:286
  132.8 33.1 %collective-permute-start.14 = (bf16[512,1280]{1,0:T(8,128)(2,1)}, bf16[512,1280]{1,0:T(8,128)(2,1)}, u32[]{:S(2)}, u32[]{:S(2)}) collective-permute-start(bf16[512,1280]{1,0:T(8,128)(2,1)} %slice.72), channel_id=1, source_target_pairs={{0,4},{2,6},{4,0},{6,2},{8,12},{10,14},{12,8},{14,10},{16,20},{18,... | collective-permute-start | bytes 3932168 | tf_op jit(solution)/shard_map/ppermute | solution.py:286
  168.8 7.2 %copy-start.2 = (bf16[512,2560]{1,0:T(8,128)(2,1)}, bf16[512,2560]{1,0:T(8,128)(2,1)S(1)}, u32[]{:S(2)}) copy-start(bf16[512,2560]{1,0:T(8,128)(2,1)S(1)} %constant_dynamic-update-slice_fusion.refs_3_) | copy-start | bytes 7864324
  168.8 7.2 %collective-permute-start.15 = (bf16[512,2560]{1,0:T(8,128)(2,1)S(1)}, bf16[512,2560]{1,0:T(8,128)(2,1)}, u32[]{:S(2)}, u32[]{:S(2)}) collective-permute-start(bf16[512,2560]{1,0:T(8,128)(2,1)S(1)} %constant_dynamic-update-slice_fusion.refs_3_), channel_id=1, source_target_pairs={{0,1},{1,0},{2,3},{3,2},{4,5},{5,4},{6,7},{7,6},{8,9},{9,8},{10,11... | collective-permute-start | bytes 7864328 | tf_op jit(solution)/shard_map/ppermute | solution.py:289
  169.1 57.8 %collective-permute-start.18 = (bf16[512,384]{1,0:T(8,128)(2,1)S(1)}, bf16[512,384]{1,0:T(8,128)(2,1)S(1)}, u32[]{:S(2)}, u32[]{:S(2)}) collective-permute-start(bf16[512,384]{1,0:T(8,128)(2,1)S(1)} %copy-done.14), channel_id=1, source_target_pairs={{0,4},{2,6},{4,0},{6,2},{8,12},{10,14},{12,8},{14,10},{16,20},{18,... | collective-permute-start | bytes 1179656 | tf_op jit(solution)/shard_map/ppermute | solution.py:286
  173.0 42.2 %collective-permute-start.16 = (bf16[512,384]{1,0:T(8,128)(2,1)}, bf16[512,384]{1,0:T(8,128)(2,1)S(1)}, u32[]{:S(2)}, u32[]{:S(2)}) collective-permute-start(bf16[512,384]{1,0:T(8,128)(2,1)} %get-tuple-element.54), channel_id=1, source_target_pairs={{0,2},{2,0},{4,6},{6,4},{8,10},{10,8},{12,14},{14,12},{16,18},{18,... | collective-permute-start | bytes 1179656 | tf_op jit(solution)/shard_map/ppermute | solution.py:286
  191.6 37.4 %collective-permute-start.20 = (bf16[512,384]{1,0:T(8,128)(2,1)}, bf16[512,384]{1,0:T(8,128)(2,1)S(1)}, u32[]{:S(2)}, u32[]{:S(2)}) collective-permute-start(bf16[512,384]{1,0:T(8,128)(2,1)} %shard_map.74), channel_id=1, source_target_pairs={{0,6},{2,4},{4,2},{6,0},{8,14},{10,12},{12,10},{14,8},{16,22},{18,... | collective-permute-start | bytes 1179656 | tf_op jit(solution)/shard_map/ppermute | solution.py:286
  215.0 11.9 %collective-permute-start.17 = (bf16[512,256]{1,0:T(8,128)(2,1)}, bf16[512,256]{1,0:T(8,128)(2,1)S(1)}, u32[]{:S(2)}, u32[]{:S(2)}) collective-permute-start(bf16[512,256]{1,0:T(8,128)(2,1)} %get-tuple-element.55), channel_id=1, source_target_pairs={{0,2},{2,0},{4,6},{6,4},{8,10},{10,8},{12,14},{14,12},{16,18},{18,... | collective-permute-start | bytes 786440 | tf_op jit(solution)/shard_map/ppermute | solution.py:286
  215.1 14.0 %collective-permute-start.19 = (bf16[512,256]{1,0:T(8,128)(2,1)}, bf16[512,256]{1,0:T(8,128)(2,1)S(1)}, u32[]{:S(2)}, u32[]{:S(2)}) collective-permute-start(bf16[512,256]{1,0:T(8,128)(2,1)} %get-tuple-element.56), channel_id=1, source_target_pairs={{0,4},{2,6},{4,0},{6,2},{8,12},{10,14},{12,8},{14,10},{16,20},{18,... | collective-permute-start | bytes 786440 | tf_op jit(solution)/shard_map/ppermute | solution.py:286
  215.1 11.7 %copy-start.8 = (bf16[512,384]{1,0:T(8,128)(2,1)}, bf16[512,384]{1,0:T(8,128)(2,1)S(1)}, u32[]{:S(2)}) copy-start(bf16[512,384]{1,0:T(8,128)(2,1)S(1)} %collective-permute-done.16.refs_2_) | copy-start | bytes 1179652
  215.1 13.9 %collective-permute-start.21 = (bf16[512,256]{1,0:T(8,128)(2,1)}, bf16[512,256]{1,0:T(8,128)(2,1)S(1)}, u32[]{:S(2)}, u32[]{:S(2)}) collective-permute-start(bf16[512,256]{1,0:T(8,128)(2,1)} %get-tuple-element.52), channel_id=1, source_target_pairs={{0,6},{2,4},{4,2},{6,0},{8,14},{10,12},{12,10},{14,8},{16,22},{18,... | collective-permute-start | bytes 786440 | tf_op jit(solution)/shard_map/ppermute | solution.py:286
  (7 other events, 14.4 us)
Sparse Core Ops, SparseCore 0:
  46.7 78.5 all-gather.2
  130.7 55.9 all-gather.4

commit v3 on v2

--- a/solution.py
+++ b/solution.py
@@ -336,7 +336,8 @@
 
     half = width // 2
     relay_y, relay_x = from_y[:, :half], from_x[:, half:]
-    from_x, from_y, relay_y, relay_x = after([from_x, from_y, relay_y, relay_x], *kv_parts)
+    from_x, from_y = after([from_x, from_y], kv_parts[3])
+    relay_y, relay_x = after([relay_y, relay_x], *kv_parts)
     corner_a, corner_b = swapped(relay_y, 1), swapped(relay_x, 2)
     token_parts = [[normed, mine_other]] + [[from_x, other_core(from_x)], [from_y, other_core(from_y)]]
 

time: 243 us -> 249 us (1.025)
  waiting for transfers between devices: 84.8 us -> 89.6 us
    ppermute x16, waiting for transfers between devices: 70.5 us -> 78.4 us  [swapped(): lax.ppermute(block, 'ctx', [(i, i ^ distance) for i in range(devices)])]
    ppermute x5, waiting for transfers between devices: 3.09 us -> 0.01 us  [other_core(): return lax.ppermute(block, 'tp', [(0, 1), (1, 0)])]
  transfers between devices with their start and end apart: 24 -> 24, of which waited for: 8 -> 7; matrix products, arithmetic and copies ran while one was open for 11% -> 12% of each run, Pallas kernels for 31% -> 30%
where the time goes in v3:
time: 249 us; the launch traced here: 245 us
  waiting for transfers between devices  89.6 us (36%)
  Pallas kernels  77.7 us (31%)
  starting transfers between devices  28.4 us (11%)
  local copies, waits for them, and re-layouts  21.8 us (9%)
  other arithmetic  14.2 us (6%)
  between operations  13.7 us (6%)
    ppermute x16, waiting for transfers between devices, swapped(): lax.ppermute(block, 'ctx', [(i, i ^ distance) for i in range(devices)])  78.4 us
    pallas_call x4, Pallas kernels, attend(): pl.pallas_call(kernel, out_shape=[jax.ShapeDtypeStruct((rows, columns), j...  74.3 us
    ppermute x16, starting transfers between devices, swapped(): lax.ppermute(block, 'ctx', [(i, i ^ distance) for i in range(devices)])  22.8 us
    ppermute x1, waiting for transfers between devices, planar(): lax.ppermute(kv_own, 'ctx', [(i, i + group) for i in range(devices - grou...  11.1 us
  transfers between devices with their start and end apart: 24, of which 7 were waited for; matrix products, arithmetic and copies ran while one was open for 12% of the time, Pallas kernels for 30%

profile of v3, /device:TPU:0, one launch (start us, length us, event | category | flops | bytes accessed | tf_op | source)
XLA Modules:
  0.0 245.3 jit_solution(13159975702455817287)
XLA Ops:
  6.5 2.6 %constant_dynamic-slice_fusion.4 = (bf16[320,640]{1,0:T(8,128)(2,1)}, bf16[320,640]{1,0:T(8,128)(2,1)}, bf16[320,640]{1,0:T(8,128)(2,1)S(1)}, bf16[320,640]{1,0:T(8,128)(2,1)}) fusion(bf16[320,2560]{1,0:T(8,128)(2,1)} %param.9, s32[]{:T(128)S(6)} %select_n.40, s32[]{:T(128)S(6)} %select_n.38, s32[]{:T(128)S(6)} %select_n.37, s32[]{:T(128)S(6)} %select_n.39), kind=kLoop, calls=%fused_computation.59 | loop fusion | bytes 3276816 | tf_op jit(solution)/shard_map/dynamic_slice | solution.py:293
  9.2 2.9 %collective-permute-start.1 = (bf16[320,640]{1,0:T(8,128)(2,1)}, bf16[320,640]{1,0:T(8,128)(2,1)}, u32[]{:S(2)}, u32[]{:S(2)}) collective-permute-start(bf16[320,640]{1,0:T(8,128)(2,1)} %get-tuple-element.58), channel_id=1, source_target_pairs={{0,2},{2,0},{4,6},{6,4},{8,10},{10,8},{12,14},{14,12},{16,18},{18,... | collective-permute-start | bytes 1228808 | tf_op jit(solution)/shard_map/ppermute | solution.py:286
  12.1 1.5 collective-permute-start.2
  13.7 1.2 fusion
  15.9 4.9 %collective-permute-start = (bf16[2,512,512]{2,1,0:T(8,128)(2,1)}, bf16[2,512,512]{2,1,0:T(8,128)(2,1)}, u32[]{:S(2)}, u32[]{:S(2)}) collective-permute-start(bf16[2,512,512]{2,1,0:T(8,128)(2,1)} %pad_maximum_fusion), channel_id=1, source_target_pairs={{0,8},{2,10},{4,12},{6,14},{8,16},{10,18},{12,20},{14,22},{16,24},... | collective-permute-start | bytes 3145736 | tf_op jit(solution)/shard_map/ppermute | solution.py:304
  22.4 2.2 fusion.2.refs_7_.refs_3_
  24.5 7.6 %collective-permute-done.2 = bf16[320,640]{1,0:T(8,128)(2,1)} collective-permute-done((bf16[320,640]{1,0:T(8,128)(2,1)}, bf16[320,640]{1,0:T(8,128)(2,1)}, u32[]{:S(2)}, u32[]{:S(2)}) %collective-permute-start.2) | collective-permute-done | bytes 409632 | tf_op jit(solution)/shard_map/ppermute | solution.py:286
  32.1 11.1 %collective-permute-done = bf16[2,512,512]{2,1,0:T(8,128)(2,1)} collective-permute-done((bf16[2,512,512]{2,1,0:T(8,128)(2,1)}, bf16[2,512,512]{2,1,0:T(8,128)(2,1)}, u32[]{:S(2)}, u32[]{:S(2)}) %collective-permute-start) | collective-permute-done | bytes 1048608 | tf_op jit(solution)/shard_map/ppermute | solution.py:304
  43.3 1.1 slice_bitcast_fusion
  45.4 1.1 pad_maximum_fusion.5
  46.6 1.6 collective-permute-start.8
  48.2 1.5 collective-permute-start.9
  49.7 1.3 reshape.35
  52.3 2.1 fusion.6
  57.4 1.4 constant_dynamic-slice_fusion
  58.8 2.3 pad_maximum_fusion.1
  61.6 56.0 %collective-permute-done.7.refs_13_.refs_9_ = bf16[2080,128]{1,0:T(8,128)(2,1)S(1)} collective-permute-done((bf16[2080,128]{1,0:T(8,128)(2,1)S(1)}, bf16[2080,128]{1,0:T(8,128)(2,1)S(1)}, u32[]{:S(2)}, u32[]{:S(2)}) %collective-permute-start.7) | collective-permute-done | bytes 532512 | tf_op jit(solution)/shard_map/ppermute | solution.py:286
  121.6 11.7 %collective-permute-done.6.refs_12_.refs_8_ = bf16[2080,128]{1,0:T(8,128)(2,1)} collective-permute-done((bf16[2080,128]{1,0:T(8,128)(2,1)}, bf16[2080,128]{1,0:T(8,128)(2,1)}, u32[]{:S(2)}, u32[]{:S(2)}) %collective-permute-start.6) | collective-permute-done | bytes 532512 | tf_op jit(solution)/shard_map/ppermute | solution.py:286
  134.7 2.5 %slice.71 = bf16[512,1280]{1,0:T(8,128)(2,1)} slice(bf16[512,2560]{1,0:T(8,128)(2,1)} %collective-permute-done.9.refs_3_.refs_5_), slice={[0:512], [0:1280]} | slice | bytes 2621440 | tf_op jit(solution)/shard_map/slice | solution.py:338
  137.2 2.5 %slice.72 = bf16[512,1280]{1,0:T(8,128)(2,1)} slice(bf16[512,2560]{1,0:T(8,128)(2,1)} %collective-permute-done.8.refs_5_.refs_7_), slice={[0:512], [1280:2560]} | slice | bytes 2621440 | tf_op jit(solution)/shard_map/slice | solution.py:338
  140.7 1.4 collective-permute-start.14
  144.1 27.2 %shard_map.73 = (bf16[512,384]{1,0:T(8,128)(2,1)}, bf16[512,384]{1,0:T(8,128)(2,1)}, bf16[512,384]{1,0:T(8,128)(2,1)}) custom-call(s32[3]{0:T(128)} %pad_add_fusion.1.refs_0_.info_ref, s32[4,6,128]{2,1,0:T(8,128)} %fusion.8.refs_1_.refs_2_, s32[4,6,128]{2,1,0:T(8,128)} %fusion.8.refs_1_.refs_2_, bf16[512,2560]{1,0:T(8,128)(2,1)} %collective-permute-done.9.refs_3_.refs_5_, ...), custom_call_target="tpu_custom_call" | custom-call | flops 8455716864 | bytes 22937600 | tf_op jit(solution)/shard_map/pallas_call | solution.py:238
  171.4 1.5 constant_dynamic-update-slice_fusion.1
  172.9 1.4 constant_dynamic-update-slice_fusion.refs_3_
  174.4 4.1 %collective-permute-start.18 = (bf16[512,384]{1,0:T(8,128)(2,1)S(1)}, bf16[512,384]{1,0:T(8,128)(2,1)S(1)}, u32[]{:S(2)}, u32[]{:S(2)}) collective-permute-start(bf16[512,384]{1,0:T(8,128)(2,1)S(1)} %copy-done.15), channel_id=1, source_target_pairs={{0,4},{2,6},{4,0},{6,2},{8,12},{10,14},{12,8},{14,10},{16,20},{18,... | collective-permute-start | bytes 1179656 | tf_op jit(solution)/shard_map/ppermute | solution.py:286
  178.4 2.7 %collective-permute-start.16 = (bf16[512,384]{1,0:T(8,128)(2,1)}, bf16[512,384]{1,0:T(8,128)(2,1)S(1)}, u32[]{:S(2)}, u32[]{:S(2)}) collective-permute-start(bf16[512,384]{1,0:T(8,128)(2,1)} %get-tuple-element.54), channel_id=1, source_target_pairs={{0,2},{2,0},{4,6},{6,4},{8,10},{10,8},{12,14},{14,12},{16,18},{18,... | collective-permute-start | bytes 1179656 | tf_op jit(solution)/shard_map/ppermute | solution.py:286
  181.1 15.5 %shard_map.74 = bf16[512,384]{1,0:T(8,128)(2,1)} custom-call(s32[3]{0:T(128)} %pad_add_fusion.1.refs_0_.info_ref, s32[4,6,128]{2,1,0:T(8,128)} %fusion.8.refs_1_.refs_2_, s32[4,6,128]{2,1,0:T(8,128)} %fusion.8.refs_1_.refs_2_, bf16[512,2560]{1,0:T(8,128)(2,1)} %copy-done.2, bf16[512,2560]{1,0:T(8,128)(2,1)} %collective-permute-done.15.refs_4_, ...), custom_call_target="tpu_custom_call" | custom-call | flops 2818572288 | bytes 11665408 | tf_op jit(solution)/shard_map/pallas_call | solution.py:238
  196.8 23.3 %shard_map.75 = (bf16[512,256]{1,0:T(8,128)(2,1)}, bf16[512,256]{1,0:T(8,128)(2,1)}, bf16[512,256]{1,0:T(8,128)(2,1)}) custom-call(s32[3]{0:T(128)} %pad_add_fusion.1.refs_0_.info_ref, s32[4,6,128]{2,1,0:T(8,128)} %fusion.8.refs_1_.refs_2_, s32[4,6,128]{2,1,0:T(8,128)} %fusion.8.refs_1_.refs_2_, bf16[512,2560]{1,0:T(8,128)(2,1)} %copy-done.2, ...), custom_call_target="tpu_custom_call" | custom-call | flops 5637144576 | bytes 21233664 | tf_op jit(solution)/shard_map/pallas_call | solution.py:238
  220.3 3.4 %collective-permute-start.21 = (bf16[512,256]{1,0:T(8,128)(2,1)}, bf16[512,256]{1,0:T(8,128)(2,1)S(1)}, u32[]{:S(2)}, u32[]{:S(2)}) collective-permute-start(bf16[512,256]{1,0:T(8,128)(2,1)} %get-tuple-element.52), channel_id=1, source_target_pairs={{0,6},{2,4},{4,2},{6,0},{8,14},{10,12},{12,10},{14,8},{16,22},{18,... | collective-permute-start | bytes 786440 | tf_op jit(solution)/shard_map/ppermute | solution.py:286
  223.6 8.3 %shard_map.76.refs_1_ = bf16[512,256]{1,0:T(8,128)(2,1)} custom-call(s32[3]{0:T(128)} %pad_add_fusion.1.refs_0_.info_ref, s32[4,6,128]{2,1,0:T(8,128)} %fusion.8.refs_1_.refs_2_, s32[4,6,128]{2,1,0:T(8,128)} %fusion.8.refs_1_.refs_2_, bf16[512,2560]{1,0:T(8,128)(2,1)} %fusion.2.refs_7_.refs_3_, bf16[512,2560]{1,0:T(8,128)(2,1)} %collective-permute-done.12.refs_8_.refs_4_, ...), custom_call_target="tpu_custom_call" | custom-call | flops 1879048192 | bytes 10223616 | tf_op jit(solution)/shard_map/pallas_call | solution.py:238
  232.0 2.1 collective-permute-done.19.refs_5_
  235.1 3.4 %shard_map.77 = bf16[512,2560]{1,0:T(8,128)(2,1)} custom-call(s32[3]{0:T(128)} %pad_add_fusion.1.refs_0_.info_ref, bf16[512,384]{1,0:T(8,128)(2,1)} %get-tuple-element.43.refs_0_, bf16[512,256]{1,0:T(8,128)(2,1)} %shard_map.76.refs_1_, bf16[512,384]{1,0:T(8,128)(2,1)} %copy-done.9, bf16[512,256]{1,0:T(8,128)(2,1)} %copy-done.11, bf16[512,384]{1,0:T(8,128)(2,1)} %copy-done.8, ...), custom_call_target="tpu_custom_call" | custom-call | bytes 5242880 | tf_op jit(solution)/shard_map/pallas_call | solution.py:374
  (83 shorter events, 18.2 us)
Async XLA Ops:
  6.5 7.1 %copy-start = (bf16[512,2560]{1,0:T(8,128)(2,1)S(1)}, bf16[512,2560]{1,0:T(8,128)(2,1)}, u32[]{:S(2)}) copy-start(bf16[512,2560]{1,0:T(8,128)(2,1)} %param.7) | copy-start | bytes 7864324
  6.5 137.6 %all-gather.3.cloned.1.call-start = ((), (), s32[]{:S(2)}) async-start(), calls=%async_computation | async-start | bytes 4915200 | tf_op jit(solution)/shard_map/all_gather | solution.py:315
  6.5 8.3 %copy-start.5 = (bf16[512,512]{1,0:T(8,128)(2,1)S(1)}, bf16[512,512]{1,0:T(8,128)(2,1)}, u32[]{:S(2)}) copy-start(bf16[512,512]{1,0:T(8,128)(2,1)} %param.10) | copy-start | bytes 1572868
  6.5 8.3 %copy-start.6 = (bf16[512,512]{1,0:T(8,128)(2,1)S(1)}, bf16[512,512]{1,0:T(8,128)(2,1)}, u32[]{:S(2)}) copy-start(bf16[512,512]{1,0:T(8,128)(2,1)} %param.11) | copy-start | bytes 1572868
  9.2 15.3 %collective-permute-start.1 = (bf16[320,640]{1,0:T(8,128)(2,1)}, bf16[320,640]{1,0:T(8,128)(2,1)}, u32[]{:S(2)}, u32[]{:S(2)}) collective-permute-start(bf16[320,640]{1,0:T(8,128)(2,1)} %get-tuple-element.58), channel_id=1, source_target_pairs={{0,2},{2,0},{4,6},{6,4},{8,10},{10,8},{12,14},{14,12},{16,18},{18,... | collective-permute-start | bytes 1228808 | tf_op jit(solution)/shard_map/ppermute | solution.py:286
  12.1 20.0 %collective-permute-start.2 = (bf16[320,640]{1,0:T(8,128)(2,1)}, bf16[320,640]{1,0:T(8,128)(2,1)}, u32[]{:S(2)}, u32[]{:S(2)}) collective-permute-start(bf16[320,640]{1,0:T(8,128)(2,1)} %get-tuple-element.60), channel_id=1, source_target_pairs={{0,4},{2,6},{4,0},{6,2},{8,12},{10,14},{12,8},{14,10},{16,20},{18,... | collective-permute-start | bytes 1228808 | tf_op jit(solution)/shard_map/ppermute | solution.py:286
  13.6 18.5 %collective-permute-start.3 = (bf16[320,640]{1,0:T(8,128)(2,1)}, bf16[320,640]{1,0:T(8,128)(2,1)}, u32[]{:S(2)}, u32[]{:S(2)}) collective-permute-start(bf16[320,640]{1,0:T(8,128)(2,1)} %get-tuple-element.57), channel_id=1, source_target_pairs={{0,6},{2,4},{4,2},{6,0},{8,14},{10,12},{12,10},{14,8},{16,22},{18,... | collective-permute-start | bytes 1228808 | tf_op jit(solution)/shard_map/ppermute | solution.py:286
  14.8 6.8 %collective-permute-start.4 = (f32[512]{0:T(512)}, f32[512]{0:T(512)}, u32[]{:S(2)}, u32[]{:S(2)}) collective-permute-start(f32[512]{0:T(512)} %fusion), channel_id=1, source_target_pairs={{0,1},{1,0},{2,3},{3,2},{4,5},{5,4},{6,7},{7,6},{8,9},{9,8},{10,11... | collective-permute-start | bytes 6152 | tf_op jit(solution)/shard_map/ppermute | solution.py:289
  15.9 27.3 %collective-permute-start = (bf16[2,512,512]{2,1,0:T(8,128)(2,1)}, bf16[2,512,512]{2,1,0:T(8,128)(2,1)}, u32[]{:S(2)}, u32[]{:S(2)}) collective-permute-start(bf16[2,512,512]{2,1,0:T(8,128)(2,1)} %pad_maximum_fusion), channel_id=1, source_target_pairs={{0,8},{2,10},{4,12},{6,14},{8,16},{10,18},{12,20},{14,22},{16,24},... | collective-permute-start | bytes 3145736 | tf_op jit(solution)/shard_map/ppermute | solution.py:304
  24.5 22.1 %copy-start.1 = (bf16[512,2560]{1,0:T(8,128)(2,1)S(1)}, bf16[512,2560]{1,0:T(8,128)(2,1)}, u32[]{:S(2)}) copy-start(bf16[512,2560]{1,0:T(8,128)(2,1)} %fusion.2.refs_7_.refs_3_) | copy-start | bytes 7864324
  46.5 150.3 %all-gather.5.cloned.1.call-start = ((), (), s32[]{:S(2)}) async-start(), calls=%async_computation.1 | async-start | bytes 3276800 | tf_op jit(solution)/shard_map/all_gather | solution.py:335
  46.6 71.0 %collective-permute-start.8 = (bf16[512,2560]{1,0:T(8,128)(2,1)S(1)}, bf16[512,2560]{1,0:T(8,128)(2,1)}, u32[]{:S(2)}, u32[]{:S(2)}) collective-permute-start(bf16[512,2560]{1,0:T(8,128)(2,1)S(1)} %copy-done.1), channel_id=1, source_target_pairs={{0,2},{2,0},{4,6},{6,4},{8,10},{10,8},{12,14},{14,12},{16,18},{18,... | collective-permute-start | bytes 7864328 | tf_op jit(solution)/shard_map/ppermute | solution.py:286
  48.2 69.7 %collective-permute-start.9 = (bf16[512,2560]{1,0:T(8,128)(2,1)S(1)}, bf16[512,2560]{1,0:T(8,128)(2,1)}, u32[]{:S(2)}, u32[]{:S(2)}) collective-permute-start(bf16[512,2560]{1,0:T(8,128)(2,1)S(1)} %copy-done.1), channel_id=1, source_target_pairs={{0,4},{2,6},{4,0},{6,2},{8,12},{10,14},{12,8},{14,10},{16,20},{18,... | collective-permute-start | bytes 7864328 | tf_op jit(solution)/shard_map/ppermute | solution.py:286
  54.4 4.4 %copy-start.14 = (bf16[32,128]{1,0:T(8,128)(2,1)S(1)}, bf16[32,128]{1,0:T(8,128)(2,1)}, u32[]{:S(2)}) copy-start(bf16[32,128]{1,0:T(8,128)(2,1)} %fusion.13) | copy-start | bytes 24580
  61.1 78.5 %copy-start.3 = (bf16[2080,128]{1,0:T(8,128)(2,1)}, bf16[2080,128]{1,0:T(8,128)(2,1)S(1)}, u32[]{:S(2)}) copy-start(bf16[2080,128]{1,0:T(8,128)(2,1)S(1)} %get-tuple-element.37.refs_10_.refs_6_) | copy-start | bytes 1597444
  61.1 56.5 %collective-permute-start.7 = (bf16[2080,128]{1,0:T(8,128)(2,1)S(1)}, bf16[2080,128]{1,0:T(8,128)(2,1)S(1)}, u32[]{:S(2)}, u32[]{:S(2)}) collective-permute-start(bf16[2080,128]{1,0:T(8,128)(2,1)S(1)} %get-tuple-element.40), channel_id=1, source_target_pairs={{0,6},{2,4},{4,2},{6,0},{8,14},{10,12},{12,10},{14,8},{16,22},{18,... | collective-permute-start | bytes 1597448 | tf_op jit(solution)/shard_map/ppermute | solution.py:286
  61.6 82.5 %collective-permute-start.12 = (bf16[512,2560]{1,0:T(8,128)(2,1)S(1)}, bf16[512,2560]{1,0:T(8,128)(2,1)}, u32[]{:S(2)}, u32[]{:S(2)}) collective-permute-start(bf16[512,2560]{1,0:T(8,128)(2,1)S(1)} %copy-done.1), channel_id=1, source_target_pairs={{0,1},{1,0},{2,3},{3,2},{4,5},{5,4},{6,7},{7,6},{8,9},{9,8},{10,11... | collective-permute-start | bytes 7864328 | tf_op jit(solution)/shard_map/ppermute | solution.py:289
  118.5 25.6 %collective-permute-start.10 = (bf16[512,2560]{1,0:T(8,128)(2,1)}, bf16[512,2560]{1,0:T(8,128)(2,1)}, u32[]{:S(2)}, u32[]{:S(2)}) collective-permute-start(bf16[512,2560]{1,0:T(8,128)(2,1)} %collective-permute-done.9.refs_3_.refs_5_), channel_id=1, source_target_pairs={{0,1},{1,0},{2,3},{3,2},{4,5},{5,4},{6,7},{7,6},{8,9},{9,8},{10,11... | collective-permute-start | bytes 7864328 | tf_op jit(solution)/shard_map/ppermute | solution.py:289
  118.5 25.6 %collective-permute-start.11 = (bf16[512,2560]{1,0:T(8,128)(2,1)}, bf16[512,2560]{1,0:T(8,128)(2,1)}, u32[]{:S(2)}, u32[]{:S(2)}) collective-permute-start(bf16[512,2560]{1,0:T(8,128)(2,1)} %collective-permute-done.8.refs_5_.refs_7_), channel_id=1, source_target_pairs={{0,1},{1,0},{2,3},{3,2},{4,5},{5,4},{6,7},{7,6},{8,9},{9,8},{10,11... | collective-permute-start | bytes 7864328 | tf_op jit(solution)/shard_map/ppermute | solution.py:289
  119.0 14.3 %collective-permute-start.6 = (bf16[2080,128]{1,0:T(8,128)(2,1)}, bf16[2080,128]{1,0:T(8,128)(2,1)}, u32[]{:S(2)}, u32[]{:S(2)}) collective-permute-start(bf16[2080,128]{1,0:T(8,128)(2,1)} %get-tuple-element.39), channel_id=1, source_target_pairs={{0,4},{2,6},{4,0},{6,2},{8,12},{10,14},{12,8},{14,10},{16,20},{18,... | collective-permute-start | bytes 1597448 | tf_op jit(solution)/shard_map/ppermute | solution.py:286
  119.9 14.0 %collective-permute-start.5 = (bf16[2080,128]{1,0:T(8,128)(2,1)}, bf16[2080,128]{1,0:T(8,128)(2,1)}, u32[]{:S(2)}, u32[]{:S(2)}) collective-permute-start(bf16[2080,128]{1,0:T(8,128)(2,1)} %get-tuple-element.38), channel_id=1, source_target_pairs={{0,2},{2,0},{4,6},{6,4},{8,10},{10,8},{12,14},{14,12},{16,18},{18,... | collective-permute-start | bytes 1597448 | tf_op jit(solution)/shard_map/ppermute | solution.py:286
  139.6 31.7 %collective-permute-start.13 = (bf16[512,1280]{1,0:T(8,128)(2,1)}, bf16[512,1280]{1,0:T(8,128)(2,1)}, u32[]{:S(2)}, u32[]{:S(2)}) collective-permute-start(bf16[512,1280]{1,0:T(8,128)(2,1)} %slice.71), channel_id=1, source_target_pairs={{0,2},{2,0},{4,6},{6,4},{8,10},{10,8},{12,14},{14,12},{16,18},{18,... | collective-permute-start | bytes 3932168 | tf_op jit(solution)/shard_map/ppermute | solution.py:286
  140.7 30.7 %collective-permute-start.14 = (bf16[512,1280]{1,0:T(8,128)(2,1)}, bf16[512,1280]{1,0:T(8,128)(2,1)}, u32[]{:S(2)}, u32[]{:S(2)}) collective-permute-start(bf16[512,1280]{1,0:T(8,128)(2,1)} %slice.72), channel_id=1, source_target_pairs={{0,4},{2,6},{4,0},{6,2},{8,12},{10,14},{12,8},{14,10},{16,20},{18,... | collective-permute-start | bytes 3932168 | tf_op jit(solution)/shard_map/ppermute | solution.py:286
  174.3 6.9 %copy-start.2 = (bf16[512,2560]{1,0:T(8,128)(2,1)}, bf16[512,2560]{1,0:T(8,128)(2,1)S(1)}, u32[]{:S(2)}) copy-start(bf16[512,2560]{1,0:T(8,128)(2,1)S(1)} %constant_dynamic-update-slice_fusion.refs_3_) | copy-start | bytes 7864324
  174.3 6.9 %collective-permute-start.15 = (bf16[512,2560]{1,0:T(8,128)(2,1)S(1)}, bf16[512,2560]{1,0:T(8,128)(2,1)}, u32[]{:S(2)}, u32[]{:S(2)}) collective-permute-start(bf16[512,2560]{1,0:T(8,128)(2,1)S(1)} %constant_dynamic-update-slice_fusion.refs_3_), channel_id=1, source_target_pairs={{0,1},{1,0},{2,3},{3,2},{4,5},{5,4},{6,7},{7,6},{8,9},{9,8},{10,11... | collective-permute-start | bytes 7864328 | tf_op jit(solution)/shard_map/ppermute | solution.py:289
  174.4 57.6 %collective-permute-start.18 = (bf16[512,384]{1,0:T(8,128)(2,1)S(1)}, bf16[512,384]{1,0:T(8,128)(2,1)S(1)}, u32[]{:S(2)}, u32[]{:S(2)}) collective-permute-start(bf16[512,384]{1,0:T(8,128)(2,1)S(1)} %copy-done.15), channel_id=1, source_target_pairs={{0,4},{2,6},{4,0},{6,2},{8,12},{10,14},{12,8},{14,10},{16,20},{18,... | collective-permute-start | bytes 1179656 | tf_op jit(solution)/shard_map/ppermute | solution.py:286
  178.4 41.8 %collective-permute-start.16 = (bf16[512,384]{1,0:T(8,128)(2,1)}, bf16[512,384]{1,0:T(8,128)(2,1)S(1)}, u32[]{:S(2)}, u32[]{:S(2)}) collective-permute-start(bf16[512,384]{1,0:T(8,128)(2,1)} %get-tuple-element.54), channel_id=1, source_target_pairs={{0,2},{2,0},{4,6},{6,4},{8,10},{10,8},{12,14},{14,12},{16,18},{18,... | collective-permute-start | bytes 1179656 | tf_op jit(solution)/shard_map/ppermute | solution.py:286
  196.7 37.4 %collective-permute-start.20 = (bf16[512,384]{1,0:T(8,128)(2,1)}, bf16[512,384]{1,0:T(8,128)(2,1)S(1)}, u32[]{:S(2)}, u32[]{:S(2)}) collective-permute-start(bf16[512,384]{1,0:T(8,128)(2,1)} %shard_map.74), channel_id=1, source_target_pairs={{0,6},{2,4},{4,2},{6,0},{8,14},{10,12},{12,10},{14,8},{16,22},{18,... | collective-permute-start | bytes 1179656 | tf_op jit(solution)/shard_map/ppermute | solution.py:286
  220.1 11.9 %collective-permute-start.17 = (bf16[512,256]{1,0:T(8,128)(2,1)}, bf16[512,256]{1,0:T(8,128)(2,1)S(1)}, u32[]{:S(2)}, u32[]{:S(2)}) collective-permute-start(bf16[512,256]{1,0:T(8,128)(2,1)} %get-tuple-element.55), channel_id=1, source_target_pairs={{0,2},{2,0},{4,6},{6,4},{8,10},{10,8},{12,14},{14,12},{16,18},{18,... | collective-permute-start | bytes 786440 | tf_op jit(solution)/shard_map/ppermute | solution.py:286
  220.2 14.0 %collective-permute-start.19 = (bf16[512,256]{1,0:T(8,128)(2,1)}, bf16[512,256]{1,0:T(8,128)(2,1)S(1)}, u32[]{:S(2)}, u32[]{:S(2)}) collective-permute-start(bf16[512,256]{1,0:T(8,128)(2,1)} %get-tuple-element.56), channel_id=1, source_target_pairs={{0,4},{2,6},{4,0},{6,2},{8,12},{10,14},{12,8},{14,10},{16,20},{18,... | collective-permute-start | bytes 786440 | tf_op jit(solution)/shard_map/ppermute | solution.py:286
  220.3 11.7 %copy-start.9 = (bf16[512,384]{1,0:T(8,128)(2,1)}, bf16[512,384]{1,0:T(8,128)(2,1)S(1)}, u32[]{:S(2)}) copy-start(bf16[512,384]{1,0:T(8,128)(2,1)S(1)} %collective-permute-done.16.refs_2_) | copy-start | bytes 1179652
  220.3 13.9 %collective-permute-start.21 = (bf16[512,256]{1,0:T(8,128)(2,1)}, bf16[512,256]{1,0:T(8,128)(2,1)S(1)}, u32[]{:S(2)}, u32[]{:S(2)}) collective-permute-start(bf16[512,256]{1,0:T(8,128)(2,1)} %get-tuple-element.52), channel_id=1, source_target_pairs={{0,6},{2,4},{4,2},{6,0},{8,14},{10,12},{12,10},{14,8},{16,22},{18,... | collective-permute-start | bytes 786440 | tf_op jit(solution)/shard_map/ppermute | solution.py:286
  (8 other events, 13.0 us)
Sparse Core Ops, SparseCore 0:
  46.7 78.5 all-gather.2
  134.1 56.3 all-gather.4

commit v4 on v2

--- a/solution.py
+++ b/solution.py
@@ -12,7 +12,7 @@
 MAXDOC = 2048
 KEYS = 512
 QUERIES = 256
-CHUNKS = 4
+CHUNKS = 2
 FAR = 1 << 30
 MASKED = -1e30
 

time: 243 us -> 244 us (level)
  the two profiles are of different devices: /device:TPU:0 before, /device:TPU:8 now
where the time goes in v4:
time: 244 us; the launch traced here: 245 us
  waiting for transfers between devices  86.3 us (35%)
  Pallas kernels  84.2 us (35%)
  starting transfers between devices  26.6 us (11%)
  local copies, waits for them, and re-layouts  21.4 us (9%)
  between operations  13.7 us (6%)
  other arithmetic  13.2 us (5%)
    pallas_call x4, Pallas kernels, attend(): pl.pallas_call(kernel, out_shape=[jax.ShapeDtypeStruct((rows, columns), j...  80.8 us
    ppermute x16, waiting for transfers between devices, swapped(): lax.ppermute(block, 'ctx', [(i, i ^ distance) for i in range(devices)])  69.4 us
    ppermute x16, starting transfers between devices, swapped(): lax.ppermute(block, 'ctx', [(i, i ^ distance) for i in range(devices)])  22.4 us
    ppermute x1, waiting for transfers between devices, planar(): lax.ppermute(kv_own, 'ctx', [(i, i + group) for i in range(devices - grou...  12 us
    slice x2, local copies, waits for them, and re-layouts, planar(): relay_y, relay_x = (from_y[:, :half], from_x[:, half:])  4.94 us
    ppermute x5, waiting for transfers between devices, other_core(): return lax.ppermute(block, 'tp', [(0, 1), (1, 0)])  4.89 us
  transfers between devices with their start and end apart: 24, of which 8 were waited for; matrix products, arithmetic and copies ran while one was open for 11% of the time, Pallas kernels for 33%

profile of v4, /device:TPU:8, one launch (start us, length us, event | category | flops | bytes accessed | tf_op | source)
XLA Modules:
  0.0 245.3 jit_solution(14937958159139579107)
XLA Ops:
  6.5 2.7 %constant_dynamic-slice_fusion.4 = (bf16[320,640]{1,0:T(8,128)(2,1)}, bf16[320,640]{1,0:T(8,128)(2,1)}, bf16[320,640]{1,0:T(8,128)(2,1)S(1)}, bf16[320,640]{1,0:T(8,128)(2,1)}) fusion(bf16[320,2560]{1,0:T(8,128)(2,1)} %param.9, s32[]{:T(128)S(6)} %select_n.40, s32[]{:T(128)S(6)} %select_n.38, s32[]{:T(128)S(6)} %select_n.37, s32[]{:T(128)S(6)} %select_n.39), kind=kLoop, calls=%fused_computation.59 | loop fusion | bytes 3276816 | tf_op jit(solution)/shard_map/dynamic_slice | solution.py:293
  9.2 1.5 collective-permute-start.1
  10.7 1.5 collective-permute-start.2
  15.0 3.5 %collective-permute-start = (bf16[2,512,512]{2,1,0:T(8,128)(2,1)}, bf16[2,512,512]{2,1,0:T(8,128)(2,1)}, u32[]{:S(2)}, u32[]{:S(2)}) collective-permute-start(bf16[2,512,512]{2,1,0:T(8,128)(2,1)} %pad_maximum_fusion), channel_id=1, source_target_pairs={{0,8},{2,10},{4,12},{6,14},{8,16},{10,18},{12,20},{14,22},{16,24},... | collective-permute-start | bytes 3145736 | tf_op jit(solution)/shard_map/ppermute | solution.py:304
  19.9 2.2 fusion.2.refs_7_.refs_3_
  22.1 8.6 %collective-permute-done.2 = bf16[320,640]{1,0:T(8,128)(2,1)} collective-permute-done((bf16[320,640]{1,0:T(8,128)(2,1)}, bf16[320,640]{1,0:T(8,128)(2,1)}, u32[]{:S(2)}, u32[]{:S(2)}) %collective-permute-start.2) | collective-permute-done | bytes 409632 | tf_op jit(solution)/shard_map/ppermute | solution.py:286
  30.7 12.0 %collective-permute-done = bf16[2,512,512]{2,1,0:T(8,128)(2,1)} collective-permute-done((bf16[2,512,512]{2,1,0:T(8,128)(2,1)}, bf16[2,512,512]{2,1,0:T(8,128)(2,1)}, u32[]{:S(2)}, u32[]{:S(2)}) %collective-permute-start) | collective-permute-done | bytes 1048608 | tf_op jit(solution)/shard_map/ppermute | solution.py:304
  46.1 1.6 collective-permute-start.9
  47.7 1.5 collective-permute-start.8
  51.8 2.2 fusion.6
  60.2 1.4 collective-permute-start.6
  61.6 1.5 collective-permute-start.5
  63.2 44.5 %collective-permute-done.9.refs_3_.refs_5_ = bf16[512,2560]{1,0:T(8,128)(2,1)} collective-permute-done((bf16[512,2560]{1,0:T(8,128)(2,1)S(1)}, bf16[512,2560]{1,0:T(8,128)(2,1)}, u32[]{:S(2)}, u32[]{:S(2)}) %collective-permute-start.9) | collective-permute-done | bytes 2621472 | tf_op jit(solution)/shard_map/ppermute | solution.py:286
  107.6 2.5 %slice.71 = bf16[512,1280]{1,0:T(8,128)(2,1)} slice(bf16[512,2560]{1,0:T(8,128)(2,1)} %collective-permute-done.9.refs_3_.refs_5_), slice={[0:512], [0:1280]} | slice | bytes 2621440 | tf_op jit(solution)/shard_map/slice | solution.py:338
  110.1 2.5 %slice.72 = bf16[512,1280]{1,0:T(8,128)(2,1)} slice(bf16[512,2560]{1,0:T(8,128)(2,1)} %collective-permute-done.8.refs_5_.refs_7_), slice={[0:512], [1280:2560]} | slice | bytes 2621440 | tf_op jit(solution)/shard_map/slice | solution.py:338
  112.6 6.4 %collective-permute-done.7.refs_13_.refs_9_ = bf16[2080,128]{1,0:T(8,128)(2,1)} collective-permute-done((bf16[2080,128]{1,0:T(8,128)(2,1)S(1)}, bf16[2080,128]{1,0:T(8,128)(2,1)}, u32[]{:S(2)}, u32[]{:S(2)}) %collective-permute-start.7) | collective-permute-done | bytes 532512 | tf_op jit(solution)/shard_map/ppermute | solution.py:286
  119.0 8.6 %collective-permute-done.6.refs_12_.refs_8_ = bf16[2080,128]{1,0:T(8,128)(2,1)} collective-permute-done((bf16[2080,128]{1,0:T(8,128)(2,1)S(1)}, bf16[2080,128]{1,0:T(8,128)(2,1)}, u32[]{:S(2)}, u32[]{:S(2)}) %collective-permute-start.6) | collective-permute-done | bytes 532512 | tf_op jit(solution)/shard_map/ppermute | solution.py:286
  130.8 1.5 collective-permute-start.13
  134.8 3.1 %collective-permute-done.11.refs_6_.refs_8_ = bf16[512,2560]{1,0:T(8,128)(2,1)} collective-permute-done((bf16[512,2560]{1,0:T(8,128)(2,1)}, bf16[512,2560]{1,0:T(8,128)(2,1)}, u32[]{:S(2)}, u32[]{:S(2)}) %collective-permute-start.11) | collective-permute-done | bytes 2621472 | tf_op jit(solution)/shard_map/ppermute | solution.py:289
  137.9 31.9 %shard_map.73 = (bf16[512,384]{1,0:T(8,128)(2,1)}, bf16[512,384]{1,0:T(8,128)(2,1)}, bf16[512,384]{1,0:T(8,128)(2,1)}) custom-call(s32[3]{0:T(128)} %pad_add_fusion.1.refs_0_.info_ref, s32[4,6,128]{2,1,0:T(8,128)} %fusion.8.refs_1_.refs_2_, s32[4,6,128]{2,1,0:T(8,128)} %fusion.8.refs_1_.refs_2_, bf16[512,2560]{1,0:T(8,128)(2,1)} %collective-permute-done.9.refs_3_.refs_5_, ...), custom_call_target="tpu_custom_call" | custom-call | flops 8455716864 | bytes 22937600 | tf_op jit(solution)/shard_map/pallas_call | solution.py:238
  169.8 1.5 constant_dynamic-update-slice_fusion.1
  171.3 1.4 constant_dynamic-update-slice_fusion.refs_3_
  173.5 2.4 collective-permute-start.16
  176.0 1.8 collective-permute-done.15.refs_4_
  177.8 14.2 %shard_map.74 = bf16[512,384]{1,0:T(8,128)(2,1)} custom-call(s32[3]{0:T(128)} %pad_add_fusion.1.refs_0_.info_ref, s32[4,6,128]{2,1,0:T(8,128)} %fusion.8.refs_1_.refs_2_, s32[4,6,128]{2,1,0:T(8,128)} %fusion.8.refs_1_.refs_2_, bf16[512,2560]{1,0:T(8,128)(2,1)} %copy-done.2, bf16[512,2560]{1,0:T(8,128)(2,1)} %collective-permute-done.15.refs_4_, ...), custom_call_target="tpu_custom_call" | custom-call | flops 2818572288 | bytes 11665408 | tf_op jit(solution)/shard_map/pallas_call | solution.py:238
  192.0 1.6 collective-permute-start.20
  193.6 22.2 %shard_map.75 = (bf16[512,256]{1,0:T(8,128)(2,1)}, bf16[512,256]{1,0:T(8,128)(2,1)}, bf16[512,256]{1,0:T(8,128)(2,1)}) custom-call(s32[3]{0:T(128)} %pad_add_fusion.1.refs_0_.info_ref, s32[4,6,128]{2,1,0:T(8,128)} %fusion.8.refs_1_.refs_2_, s32[4,6,128]{2,1,0:T(8,128)} %fusion.8.refs_1_.refs_2_, bf16[512,2560]{1,0:T(8,128)(2,1)} %copy-done.2, ...), custom_call_target="tpu_custom_call" | custom-call | flops 5637144576 | bytes 21233664 | tf_op jit(solution)/shard_map/pallas_call | solution.py:238
  215.8 1.9 collective-permute-start.17
  217.7 2.2 collective-permute-start.19
  219.9 1.5 collective-permute-start.21
  221.3 12.6 %shard_map.76.refs_1_ = bf16[512,256]{1,0:T(8,128)(2,1)} custom-call(s32[3]{0:T(128)} %pad_add_fusion.1.refs_0_.info_ref, s32[4,6,128]{2,1,0:T(8,128)} %fusion.8.refs_1_.refs_2_, s32[4,6,128]{2,1,0:T(8,128)} %fusion.8.refs_1_.refs_2_, bf16[512,2560]{1,0:T(8,128)(2,1)} %fusion.2.refs_7_.refs_3_, bf16[512,2560]{1,0:T(8,128)(2,1)} %collective-permute-done.12.refs_8_.refs_4_, ...), custom_call_target="tpu_custom_call" | custom-call | flops 1879048192 | bytes 10223616 | tf_op jit(solution)/shard_map/pallas_call | solution.py:238
  235.1 3.4 %shard_map.77 = bf16[512,2560]{1,0:T(8,128)(2,1)} custom-call(s32[3]{0:T(128)} %pad_add_fusion.1.refs_0_.info_ref, bf16[512,384]{1,0:T(8,128)(2,1)} %get-tuple-element.43.refs_0_, bf16[512,256]{1,0:T(8,128)(2,1)} %shard_map.76.refs_1_, bf16[512,384]{1,0:T(8,128)(2,1)} %copy-done.8, bf16[512,256]{1,0:T(8,128)(2,1)} %copy-done.10, bf16[512,384]{1,0:T(8,128)(2,1)} %copy-done.7, ...), custom_call_target="tpu_custom_call" | custom-call | bytes 5242880 | tf_op jit(solution)/shard_map/pallas_call | solution.py:373
  (81 shorter events, 24.1 us)
Async XLA Ops:
  6.5 6.2 %copy-start = (bf16[512,2560]{1,0:T(8,128)(2,1)S(1)}, bf16[512,2560]{1,0:T(8,128)(2,1)}, u32[]{:S(2)}) copy-start(bf16[512,2560]{1,0:T(8,128)(2,1)} %param.7) | copy-start | bytes 7864324
  6.5 131.3 %all-gather.3.cloned.1.call-start = ((), (), s32[]{:S(2)}) async-start(), calls=%async_computation | async-start | bytes 4915200 | tf_op jit(solution)/shard_map/all_gather | solution.py:315
  6.5 7.3 %copy-start.4 = (bf16[512,512]{1,0:T(8,128)(2,1)S(1)}, bf16[512,512]{1,0:T(8,128)(2,1)}, u32[]{:S(2)}) copy-start(bf16[512,512]{1,0:T(8,128)(2,1)} %param.10) | copy-start | bytes 1572868
  6.5 7.3 %copy-start.5 = (bf16[512,512]{1,0:T(8,128)(2,1)S(1)}, bf16[512,512]{1,0:T(8,128)(2,1)}, u32[]{:S(2)}) copy-start(bf16[512,512]{1,0:T(8,128)(2,1)} %param.11) | copy-start | bytes 1572868
  9.2 12.9 %collective-permute-start.1 = (bf16[320,640]{1,0:T(8,128)(2,1)}, bf16[320,640]{1,0:T(8,128)(2,1)}, u32[]{:S(2)}, u32[]{:S(2)}) collective-permute-start(bf16[320,640]{1,0:T(8,128)(2,1)} %get-tuple-element.58), channel_id=1, source_target_pairs={{0,2},{2,0},{4,6},{6,4},{8,10},{10,8},{12,14},{14,12},{16,18},{18,... | collective-permute-start | bytes 1228808 | tf_op jit(solution)/shard_map/ppermute | solution.py:286
  10.7 20.0 %collective-permute-start.2 = (bf16[320,640]{1,0:T(8,128)(2,1)}, bf16[320,640]{1,0:T(8,128)(2,1)}, u32[]{:S(2)}, u32[]{:S(2)}) collective-permute-start(bf16[320,640]{1,0:T(8,128)(2,1)} %get-tuple-element.60), channel_id=1, source_target_pairs={{0,4},{2,6},{4,0},{6,2},{8,12},{10,14},{12,8},{14,10},{16,20},{18,... | collective-permute-start | bytes 1228808 | tf_op jit(solution)/shard_map/ppermute | solution.py:286
  12.2 18.5 %collective-permute-start.3 = (bf16[320,640]{1,0:T(8,128)(2,1)}, bf16[320,640]{1,0:T(8,128)(2,1)}, u32[]{:S(2)}, u32[]{:S(2)}) collective-permute-start(bf16[320,640]{1,0:T(8,128)(2,1)} %get-tuple-element.57), channel_id=1, source_target_pairs={{0,6},{2,4},{4,2},{6,0},{8,14},{10,12},{12,10},{14,8},{16,22},{18,... | collective-permute-start | bytes 1228808 | tf_op jit(solution)/shard_map/ppermute | solution.py:286
  13.9 5.4 %collective-permute-start.4 = (f32[512]{0:T(512)}, f32[512]{0:T(512)}, u32[]{:S(2)}, u32[]{:S(2)}) collective-permute-start(f32[512]{0:T(512)} %fusion), channel_id=1, source_target_pairs={{0,1},{1,0},{2,3},{3,2},{4,5},{5,4},{6,7},{7,6},{8,9},{9,8},{10,11... | collective-permute-start | bytes 6152 | tf_op jit(solution)/shard_map/ppermute | solution.py:289
  15.0 27.8 %collective-permute-start = (bf16[2,512,512]{2,1,0:T(8,128)(2,1)}, bf16[2,512,512]{2,1,0:T(8,128)(2,1)}, u32[]{:S(2)}, u32[]{:S(2)}) collective-permute-start(bf16[2,512,512]{2,1,0:T(8,128)(2,1)} %pad_maximum_fusion), channel_id=1, source_target_pairs={{0,8},{2,10},{4,12},{6,14},{8,16},{10,18},{12,20},{14,22},{16,24},... | collective-permute-start | bytes 3145736 | tf_op jit(solution)/shard_map/ppermute | solution.py:304
  22.1 24.0 %copy-start.1 = (bf16[512,2560]{1,0:T(8,128)(2,1)S(1)}, bf16[512,2560]{1,0:T(8,128)(2,1)}, u32[]{:S(2)}) copy-start(bf16[512,2560]{1,0:T(8,128)(2,1)} %fusion.2.refs_7_.refs_3_) | copy-start | bytes 7864324
  46.0 147.6 %all-gather.5.cloned.1.call-start = ((), (), s32[]{:S(2)}) async-start(), calls=%async_computation.1 | async-start | bytes 3276800 | tf_op jit(solution)/shard_map/all_gather | solution.py:335
  46.1 61.5 %collective-permute-start.9 = (bf16[512,2560]{1,0:T(8,128)(2,1)S(1)}, bf16[512,2560]{1,0:T(8,128)(2,1)}, u32[]{:S(2)}, u32[]{:S(2)}) collective-permute-start(bf16[512,2560]{1,0:T(8,128)(2,1)S(1)} %copy-done.1), channel_id=1, source_target_pairs={{0,4},{2,6},{4,0},{6,2},{8,12},{10,14},{12,8},{14,10},{16,20},{18,... | collective-permute-start | bytes 7864328 | tf_op jit(solution)/shard_map/ppermute | solution.py:286
  47.7 62.4 %collective-permute-start.8 = (bf16[512,2560]{1,0:T(8,128)(2,1)S(1)}, bf16[512,2560]{1,0:T(8,128)(2,1)}, u32[]{:S(2)}, u32[]{:S(2)}) collective-permute-start(bf16[512,2560]{1,0:T(8,128)(2,1)S(1)} %copy-done.1), channel_id=1, source_target_pairs={{0,2},{2,0},{4,6},{6,4},{8,10},{10,8},{12,14},{14,12},{16,18},{18,... | collective-permute-start | bytes 7864328 | tf_op jit(solution)/shard_map/ppermute | solution.py:286
  53.9 4.4 %copy-start.13 = (bf16[32,128]{1,0:T(8,128)(2,1)S(1)}, bf16[32,128]{1,0:T(8,128)(2,1)}, u32[]{:S(2)}) copy-start(bf16[32,128]{1,0:T(8,128)(2,1)} %fusion.13) | copy-start | bytes 24580
  59.6 70.4 %copy-start.3 = (bf16[2080,128]{1,0:T(8,128)(2,1)}, bf16[2080,128]{1,0:T(8,128)(2,1)S(1)}, u32[]{:S(2)}) copy-start(bf16[2080,128]{1,0:T(8,128)(2,1)S(1)} %get-tuple-element.37.refs_10_.refs_6_) | copy-start | bytes 1597444
  59.6 59.4 %collective-permute-start.7 = (bf16[2080,128]{1,0:T(8,128)(2,1)S(1)}, bf16[2080,128]{1,0:T(8,128)(2,1)}, u32[]{:S(2)}, u32[]{:S(2)}) collective-permute-start(bf16[2080,128]{1,0:T(8,128)(2,1)S(1)} %get-tuple-element.40), channel_id=1, source_target_pairs={{0,6},{2,4},{4,2},{6,0},{8,14},{10,12},{12,10},{14,8},{16,22},{18,... | collective-permute-start | bytes 1597448 | tf_op jit(solution)/shard_map/ppermute | solution.py:286
  60.2 67.3 %collective-permute-start.6 = (bf16[2080,128]{1,0:T(8,128)(2,1)S(1)}, bf16[2080,128]{1,0:T(8,128)(2,1)}, u32[]{:S(2)}, u32[]{:S(2)}) collective-permute-start(bf16[2080,128]{1,0:T(8,128)(2,1)S(1)} %get-tuple-element.39), channel_id=1, source_target_pairs={{0,4},{2,6},{4,0},{6,2},{8,12},{10,14},{12,8},{14,10},{16,20},{18,... | collective-permute-start | bytes 1597448 | tf_op jit(solution)/shard_map/ppermute | solution.py:286
  61.6 67.2 %collective-permute-start.5 = (bf16[2080,128]{1,0:T(8,128)(2,1)S(1)}, bf16[2080,128]{1,0:T(8,128)(2,1)}, u32[]{:S(2)}, u32[]{:S(2)}) collective-permute-start(bf16[2080,128]{1,0:T(8,128)(2,1)S(1)} %get-tuple-element.38), channel_id=1, source_target_pairs={{0,2},{2,0},{4,6},{6,4},{8,10},{10,8},{12,14},{14,12},{16,18},{18,... | collective-permute-start | bytes 1597448 | tf_op jit(solution)/shard_map/ppermute | solution.py:286
  107.6 27.2 %collective-permute-start.12 = (bf16[512,2560]{1,0:T(8,128)(2,1)S(1)}, bf16[512,2560]{1,0:T(8,128)(2,1)}, u32[]{:S(2)}, u32[]{:S(2)}) collective-permute-start(bf16[512,2560]{1,0:T(8,128)(2,1)S(1)} %copy-done.1), channel_id=1, source_target_pairs={{0,1},{1,0},{2,3},{3,2},{4,5},{5,4},{6,7},{7,6},{8,9},{9,8},{10,11... | collective-permute-start | bytes 7864328 | tf_op jit(solution)/shard_map/ppermute | solution.py:289
  128.9 5.9 %collective-permute-start.10 = (bf16[512,2560]{1,0:T(8,128)(2,1)}, bf16[512,2560]{1,0:T(8,128)(2,1)}, u32[]{:S(2)}, u32[]{:S(2)}) collective-permute-start(bf16[512,2560]{1,0:T(8,128)(2,1)} %collective-permute-done.9.refs_3_.refs_5_), channel_id=1, source_target_pairs={{0,1},{1,0},{2,3},{3,2},{4,5},{5,4},{6,7},{7,6},{8,9},{9,8},{10,11... | collective-permute-start | bytes 7864328 | tf_op jit(solution)/shard_map/ppermute | solution.py:289
  128.9 9.0 %collective-permute-start.11 = (bf16[512,2560]{1,0:T(8,128)(2,1)}, bf16[512,2560]{1,0:T(8,128)(2,1)}, u32[]{:S(2)}, u32[]{:S(2)}) collective-permute-start(bf16[512,2560]{1,0:T(8,128)(2,1)} %collective-permute-done.8.refs_5_.refs_7_), channel_id=1, source_target_pairs={{0,1},{1,0},{2,3},{3,2},{4,5},{5,4},{6,7},{7,6},{8,9},{9,8},{10,11... | collective-permute-start | bytes 7864328 | tf_op jit(solution)/shard_map/ppermute | solution.py:289
  130.8 39.0 %collective-permute-start.13 = (bf16[512,1280]{1,0:T(8,128)(2,1)}, bf16[512,1280]{1,0:T(8,128)(2,1)}, u32[]{:S(2)}, u32[]{:S(2)}) collective-permute-start(bf16[512,1280]{1,0:T(8,128)(2,1)} %slice.71), channel_id=1, source_target_pairs={{0,2},{2,0},{4,6},{6,4},{8,10},{10,8},{12,14},{14,12},{16,18},{18,... | collective-permute-start | bytes 3932168 | tf_op jit(solution)/shard_map/ppermute | solution.py:286
  132.2 37.5 %collective-permute-start.14 = (bf16[512,1280]{1,0:T(8,128)(2,1)}, bf16[512,1280]{1,0:T(8,128)(2,1)}, u32[]{:S(2)}, u32[]{:S(2)}) collective-permute-start(bf16[512,1280]{1,0:T(8,128)(2,1)} %slice.72), channel_id=1, source_target_pairs={{0,4},{2,6},{4,0},{6,2},{8,12},{10,14},{12,8},{14,10},{16,20},{18,... | collective-permute-start | bytes 3932168 | tf_op jit(solution)/shard_map/ppermute | solution.py:286
  172.7 5.1 %copy-start.2 = (bf16[512,2560]{1,0:T(8,128)(2,1)}, bf16[512,2560]{1,0:T(8,128)(2,1)S(1)}, u32[]{:S(2)}) copy-start(bf16[512,2560]{1,0:T(8,128)(2,1)S(1)} %constant_dynamic-update-slice_fusion.refs_3_) | copy-start | bytes 7864324
  172.7 5.1 %collective-permute-start.15 = (bf16[512,2560]{1,0:T(8,128)(2,1)S(1)}, bf16[512,2560]{1,0:T(8,128)(2,1)}, u32[]{:S(2)}, u32[]{:S(2)}) collective-permute-start(bf16[512,2560]{1,0:T(8,128)(2,1)S(1)} %constant_dynamic-update-slice_fusion.refs_3_), channel_id=1, source_target_pairs={{0,1},{1,0},{2,3},{3,2},{4,5},{5,4},{6,7},{7,6},{8,9},{9,8},{10,11... | collective-permute-start | bytes 7864328 | tf_op jit(solution)/shard_map/ppermute | solution.py:289
  172.9 61.0 %collective-permute-start.18 = (bf16[512,384]{1,0:T(8,128)(2,1)S(1)}, bf16[512,384]{1,0:T(8,128)(2,1)S(1)}, u32[]{:S(2)}, u32[]{:S(2)}) collective-permute-start(bf16[512,384]{1,0:T(8,128)(2,1)S(1)} %copy-done.14), channel_id=1, source_target_pairs={{0,4},{2,6},{4,0},{6,2},{8,12},{10,14},{12,8},{14,10},{16,20},{18,... | collective-permute-start | bytes 1179656 | tf_op jit(solution)/shard_map/ppermute | solution.py:286
  173.5 46.3 %collective-permute-start.16 = (bf16[512,384]{1,0:T(8,128)(2,1)}, bf16[512,384]{1,0:T(8,128)(2,1)S(1)}, u32[]{:S(2)}, u32[]{:S(2)}) collective-permute-start(bf16[512,384]{1,0:T(8,128)(2,1)} %get-tuple-element.54), channel_id=1, source_target_pairs={{0,2},{2,0},{4,6},{6,4},{8,10},{10,8},{12,14},{14,12},{16,18},{18,... | collective-permute-start | bytes 1179656 | tf_op jit(solution)/shard_map/ppermute | solution.py:286
  192.0 42.0 %collective-permute-start.20 = (bf16[512,384]{1,0:T(8,128)(2,1)}, bf16[512,384]{1,0:T(8,128)(2,1)S(1)}, u32[]{:S(2)}, u32[]{:S(2)}) collective-permute-start(bf16[512,384]{1,0:T(8,128)(2,1)} %shard_map.74), channel_id=1, source_target_pairs={{0,6},{2,4},{4,2},{6,0},{8,14},{10,12},{12,10},{14,8},{16,22},{18,... | collective-permute-start | bytes 1179656 | tf_op jit(solution)/shard_map/ppermute | solution.py:286
  215.8 18.1 %collective-permute-start.17 = (bf16[512,256]{1,0:T(8,128)(2,1)}, bf16[512,256]{1,0:T(8,128)(2,1)S(1)}, u32[]{:S(2)}, u32[]{:S(2)}) collective-permute-start(bf16[512,256]{1,0:T(8,128)(2,1)} %get-tuple-element.55), channel_id=1, source_target_pairs={{0,2},{2,0},{4,6},{6,4},{8,10},{10,8},{12,14},{14,12},{16,18},{18,... | collective-permute-start | bytes 786440 | tf_op jit(solution)/shard_map/ppermute | solution.py:286
  217.7 16.3 %collective-permute-start.19 = (bf16[512,256]{1,0:T(8,128)(2,1)}, bf16[512,256]{1,0:T(8,128)(2,1)S(1)}, u32[]{:S(2)}, u32[]{:S(2)}) collective-permute-start(bf16[512,256]{1,0:T(8,128)(2,1)} %get-tuple-element.56), channel_id=1, source_target_pairs={{0,4},{2,6},{4,0},{6,2},{8,12},{10,14},{12,8},{14,10},{16,20},{18,... | collective-permute-start | bytes 786440 | tf_op jit(solution)/shard_map/ppermute | solution.py:286
  219.9 14.0 %copy-start.8 = (bf16[512,384]{1,0:T(8,128)(2,1)}, bf16[512,384]{1,0:T(8,128)(2,1)S(1)}, u32[]{:S(2)}) copy-start(bf16[512,384]{1,0:T(8,128)(2,1)S(1)} %collective-permute-done.16.refs_2_) | copy-start | bytes 1179652
  219.9 14.1 %collective-permute-start.21 = (bf16[512,256]{1,0:T(8,128)(2,1)}, bf16[512,256]{1,0:T(8,128)(2,1)S(1)}, u32[]{:S(2)}, u32[]{:S(2)}) collective-permute-start(bf16[512,256]{1,0:T(8,128)(2,1)} %get-tuple-element.52), channel_id=1, source_target_pairs={{0,6},{2,4},{4,2},{6,0},{8,14},{10,12},{12,10},{14,8},{16,22},{18,... | collective-permute-start | bytes 786440 | tf_op jit(solution)/shard_map/ppermute | solution.py:286
  (7 other events, 12.0 us)
Sparse Core Ops, SparseCore 0:
  46.1 74.9 all-gather.2
  130.2 53.1 all-gather.4
